TPU v7x, 32 devices: a whole 2x2x4 slice. The times are simulated.
32 devices in a mesh: groups: 2 (over y), expert: 8 (over z, core), section: 2 (over x), tensor: 1.
Axes of the slice: x: 2, y: 2, z: 4, core: 2. Of those that a mesh axis runs over, the one named last changes fastest.
Arguments:
- opening_residual: bfloat16 [2, 2048, 2048], P('section', ('groups', 'expert'), 'tensor'), parts along dimension 1, may hold values from -12 to 12
- incoming_residual: bfloat16 [1, 2048, 2048], P(None, ('groups', 'expert'), 'tensor'), parts along dimension 1, may hold values from -12 to 12
- stored_summaries: bfloat16 [2, 2, 16, 768, 512], P(None, 'section', ('groups', 'expert')), parts along dimension 2, may hold values from -40 to 40
- stored_counts: int32 [3, 16], P(None, ('groups', 'expert')), parts along dimension 1, may hold values from 1 to 768, as said below
- picked_specialists: int32 [2, 2, 2048, 6], P(None, 'section', ('groups', 'expert')), parts along dimension 2, may hold values from 0 to 15, all different within a row; in each aligned block of 128 rows (0 to 127, 128 to 255, ..., all dimensions but the last counted through in order) at most 64 rows name the same one
- chooser_mixing_share: float32 [2, 2, 2048, 6], P(None, 'section', ('groups', 'expert')), parts along dimension 2, may hold values from 0.05 to 0.4
- mixing_scale_factor: float32 [2, 2048], P('section'), may hold values from 0.25 to 1.75
- asking_projection: bfloat16 [2, 2048, 1024], P('section', None, 'tensor'), may hold values from -0.125 to 0.125
- summary_lookup_factor: bfloat16 [2, 8, 128, 512], P('section', 'tensor'), may hold values from -0.5 to 0.5
- summary_content_factor: bfloat16 [2, 8, 512, 128], P('section', 'tensor'), may hold values from -0.25 to 0.25
- merging_projection: bfloat16 [2, 1024, 2048], P('section', 'tensor'), may hold values from -0.1875 to 0.1875
- compress_projection: bfloat16 [2, 2048, 512], P('section', None, 'tensor'), may hold values from -0.125 to 0.125
- summary_scale_factor: float32 [2, 512], P('section'), may hold values from 0.25 to 1.75
- specialist_scale_factor: float32 [2, 2048], P('section', 'tensor'), may hold values from 0.25 to 1.75
- specialist_switch_factor: bfloat16 [2, 16, 2048, 704], P('section', 'expert', None, 'tensor'), may hold values from -0.125 to 0.125
- specialist_widen_factor: bfloat16 [2, 16, 2048, 704], P('section', 'expert', None, 'tensor'), may hold values from -0.125 to 0.125
- specialist_contract_factor: bfloat16 [2, 16, 704, 2048], P('section', 'expert', 'tensor'), may hold values from -0.21875 to 0.21875
Outputs:
- results: bfloat16 [2, 2, 2048, 2048], P(None, 'section', ('groups', 'expert'), 'tensor'), parts along dimension 2
There are 2 independent parts, one for each index of `groups`. A program takes and returns all parts, laid end to end along the dimension named above; an argument that names none is the same for every part. Nothing has to cross between parts.
Inputs may be any that keep to these rules, and one draw needn't show every extreme that they name: `picked_specialists`: in each aligned block of 128 rows (one sequence) no expert is chosen by more than 64 rows, a bound that some block reaches; each row names 6 different experts. `stored_counts`: in every microbatch some sequence has exactly 768 cached tokens.
All inputs are finite; a program needn't handle non-finite values.
Results may differ from a plain program's by a relative error of at most 0.04.
Values may be sent and summed in bfloat16 or wider, within the bound.
A program may use at most 128 MiB of HBM per device.

v0:
```python
import jax
import jax.numpy as jnp
from jax import lax
from jax.sharding import PartitionSpec as P

EXPERTS = 16
CAP = 64


epsilon = 1e-06


def shifted(value, axis, steps):
    count = lax.axis_size(axis)
    initial, last = (max(0, -steps), min(count, count - steps))
    return lax.ppermute(value, axis, [(source, source + steps) for source in range(initial, last)])


def row_norm(values, gain_row):
    return (
        values * lax.rsqrt(jnp.mean(values * values, axis=-1, keepdims=True) + epsilon) * gain_row
    )


def attend(q_lat, cache_rows, new_rows, length, score_scale):
    piece_list = q_lat.shape[0]
    context = cache_rows.shape[0]
    key_rows = jnp.concatenate([cache_rows, new_rows], axis=0)
    scores = (
        jnp.einsum("thl,kl->thk", q_lat, key_rows, preferred_element_type=jnp.float32) * score_scale
    )
    position = lax.broadcasted_iota(jnp.int32, (piece_list, context + piece_list), 1)
    query_pos = lax.broadcasted_iota(jnp.int32, (piece_list, context + piece_list), 0)
    visible = jnp.where(position < context, position < length, position - context <= query_pos)
    scores = jnp.where(visible[:, None, :], scores, -jnp.inf)
    row_max = jnp.max(scores, axis=-1, keepdims=True)
    expd = jnp.where(visible[:, None, :], jnp.exp(scores - row_max), 0.0)
    attention = (expd / jnp.sum(expd, axis=-1, keepdims=True)).astype(jnp.bfloat16)
    return jnp.einsum(
        "thk,kl->thl", attention, key_rows, preferred_element_type=jnp.float32
    ).astype(jnp.bfloat16)


def shards(
    opening_residual,
    incoming_residual,
    stored_summaries,
    stored_counts,
    picked_specialists,
    chooser_mixing_share,
    mixing_scale_factor,
    asking_projection,
    summary_lookup_factor,
    summary_content_factor,
    merging_projection,
    compress_projection,
    summary_scale_factor,
    specialist_scale_factor,
    specialist_switch_factor,
    specialist_widen_factor,
    specialist_contract_factor,
):
    segment_ordinal = lax.axis_index("section")
    section_count = lax.axis_size("section")
    sources = lax.axis_size("expert")
    tick_count = stored_summaries.shape[0]
    piece_list = opening_residual.shape[1]
    inner_feature_midcount = opening_residual.shape[2]
    full_width = mixing_scale_factor.shape[1]
    local_heads = summary_lookup_factor.shape[1]
    head_size = summary_lookup_factor.shape[2]
    top_count = picked_specialists.shape[3]
    expert_local = specialist_switch_factor.shape[1]
    score_scale = head_size ** (-0.5)
    outputs = []
    present_carry = opening_residual[0]
    section_out = present_carry
    for step_index in range(tick_count):
        if step_index > 0:
            handed = shifted(section_out, "section", 1)
            present_carry = jnp.where(
                segment_ordinal == 0, incoming_residual[step_index - 1], handed
            )
        micro_index = step_index - segment_ordinal + section_count - 1
        length = lax.dynamic_index_in_dim(stored_counts[:, 0], micro_index, 0, keepdims=False)
        full_rows = lax.all_gather(present_carry, "tensor", axis=1, tiled=True)
        normed = row_norm(full_rows.astype(jnp.float32), mixing_scale_factor[0]).astype(
            jnp.bfloat16
        )
        queries = jnp.dot(normed, asking_projection[0], preferred_element_type=jnp.float32).astype(
            jnp.bfloat16
        )
        queries = queries.reshape(piece_list, local_heads, head_size)
        q_lat = jnp.einsum(
            "thd,hdl->thl", queries, summary_lookup_factor[0], preferred_element_type=jnp.float32
        ).astype(jnp.bfloat16)
        latent_part = jnp.dot(normed, compress_projection[0], preferred_element_type=jnp.float32)
        latent_raw = lax.all_gather(
            latent_part.astype(jnp.bfloat16), "tensor", axis=1, tiled=True
        ).astype(latent_part.dtype)
        new_latent = row_norm(latent_raw, summary_scale_factor[0]).astype(jnp.bfloat16)
        o_lat = attend(q_lat, stored_summaries[step_index, 0, 0], new_latent, length, score_scale)
        heads_out = jnp.einsum(
            "thl,hld->thd", o_lat, summary_content_factor[0], preferred_element_type=jnp.float32
        ).astype(jnp.bfloat16)
        heads_out = heads_out.reshape(piece_list, local_heads * head_size)
        head_terms = jnp.dot(heads_out, merging_projection[0], preferred_element_type=jnp.float32)
        residual = present_carry.astype(jnp.float32) + lax.psum_scatter(
            head_terms.astype(jnp.bfloat16), "tensor", scatter_dimension=1, tiled=True
        ).astype(jnp.float32)
        squares = lax.psum(jnp.sum(residual * residual, axis=1), "tensor")
        moe_input = (
            residual
            * lax.rsqrt(squares / full_width + epsilon)[:, None]
            * specialist_scale_factor[0]
        ).astype(jnp.bfloat16)
        choices = picked_specialists[step_index, 0].reshape(-1)
        onehot = (choices[:, None] == lax.broadcasted_iota(jnp.int32, (1, EXPERTS), 1)).astype(
            jnp.int32
        )
        earlier = jnp.cumsum(onehot, axis=0) - onehot
        slot_index = jnp.sum(earlier * onehot, axis=1)
        target = choices * CAP + slot_index
        owner_row = lax.broadcasted_iota(jnp.int32, (piece_list, top_count), 0).reshape(-1)
        source = jnp.full((EXPERTS * CAP,), piece_list, jnp.int32).at[target].set(owner_row)
        whole_rows = lax.all_gather(moe_input, "tensor", axis=1, tiled=True)
        padded = jnp.concatenate([whole_rows, jnp.zeros((1, full_width), jnp.bfloat16)], axis=0)
        outbox = padded[source].reshape(EXPERTS, CAP, full_width)
        received = lax.all_to_all(outbox, "expert", split_axis=0, concat_axis=0, tiled=True)
        item_count = received.shape[1]
        grouped = received.reshape(sources, expert_local, item_count, full_width)
        serve_gate_values = jnp.einsum(
            "jend,edf->jenf",
            grouped,
            specialist_switch_factor[0],
            preferred_element_type=jnp.float32,
        )
        serve_up_values = jnp.einsum(
            "jend,edf->jenf",
            grouped,
            specialist_widen_factor[0],
            preferred_element_type=jnp.float32,
        )
        hidden = (jax.nn.silu(serve_gate_values) * serve_up_values).astype(jnp.bfloat16)
        partial_value = jnp.einsum(
            "jenf,efd->jend",
            hidden,
            specialist_contract_factor[0],
            preferred_element_type=jnp.float32,
        ).astype(jnp.bfloat16)
        partial_value = partial_value.reshape(sources * expert_local, item_count, full_width)
        returned = lax.all_to_all(partial_value, "expert", split_axis=0, concat_axis=0, tiled=True)
        expert_out = lax.psum_scatter(
            returned.astype(jnp.float32).astype(jnp.bfloat16),
            "tensor",
            scatter_dimension=2,
            tiled=True,
        )
        picked = expert_out.reshape(EXPERTS * CAP, inner_feature_midcount)[target].astype(
            jnp.float32
        )
        picked = picked.reshape(piece_list, top_count, inner_feature_midcount)
        routed = jnp.sum(picked * chooser_mixing_share[step_index, 0][:, :, None], axis=1)
        section_out = (residual + routed).astype(jnp.bfloat16)
        outputs.append(section_out)
    return jnp.stack(outputs)[:, None]


def solution(mesh):
    in_specs = (
        P("section", ("groups", "expert"), "tensor"),
        P(None, ("groups", "expert"), "tensor"),
        P(None, "section", ("groups", "expert"), None, None),
        P(None, ("groups", "expert")),
        P(None, "section", ("groups", "expert"), None),
        P(None, "section", ("groups", "expert"), None),
        P("section", None),
        P("section", None, "tensor"),
        P("section", "tensor", None, None),
        P("section", "tensor", None, None),
        P("section", "tensor", None),
        P("section", None, "tensor"),
        P("section", None),
        P("section", "tensor"),
        P("section", "expert", None, "tensor"),
        P("section", "expert", None, "tensor"),
        P("section", "expert", "tensor", None),
    )
    out_specs = P(None, "section", ("groups", "expert"), "tensor")
    return jax.shard_map(shards, mesh=mesh, in_specs=in_specs, out_specs=out_specs, check_vma=False)
```

profile of v0, /device:TPU:10, one launch (start us, length us, event | category | flops | bytes accessed | tf_op | source)
XLA Modules:
  0.0 586.6 jit_solution(10285239490774772103)
XLA Ops:
  20.2 6.8 %fusion.181 = (f32[128,8]{0,1:T(8,128)S(1)}, f32[128,8,896]{2,0,1:T(8,128)}) fusion(f32[128,8,896]{2,0,1:T(8,128)} %fusion.91, pred[128,896]{1,0:T(8,128)(4,1)} %get-tuple-element.16), kind=kOutput, calls=%fused_computation.196 | output fusion | flops 6423423 | bytes 7458816 | tf_op jit(solution)/shard_map/sub | solution.py:37
  40.3 6.0 %gather_fusion = bf16[1024,2048]{1,0:T(8,128)(2,1)} fusion(bf16[129,2048]{1,0:T(8,128)(2,1)S(1)} %concatenate.13, s32[1024]{0:T(1024)S(1)} %fusion.159), kind=kCustom, calls=%fused_computation | custom fusion | bytes 8392704 | tf_op jit(solution)/shard_map/gather | solution.py:128
  46.4 97.6 %all_to_all.20 = bf16[16,64,2048]{2,1,0:T(8,128)(2,1)S(1)} all-to-all(bf16[16,64,2048]{2,1,0:T(8,128)(2,1)} %bitcast.278), channel_id=1, replica_groups=mesh['groups'=2,'expert'=8,'section'=2,'tensor'=1] {'expert'}, dimensions={0} | all-to-all | bytes 8388608 | tf_op jit(solution)/shard_map/all_to_all | solution.py:129
  145.9 7.8 %fusion.8 = f32[2,8,64,704]{3,2,1,0:T(8,128)} fusion(bf16[1,2,2048,704]{2,3,1,0:T(8,128)(2,1)} %param.32, bf16[8,2,64,2048]{3,2,1,0:T(8,128)(2,1)S(1)} %bitcast.282), kind=kOutput, calls=%fused_computation.16 | convolution fusion | flops 2952790016 | bytes 12845056 | tf_op jit(solution)/shard_map/jend,edf->jenf/dot_general | solution.py:138
  153.8 13.1 %convert_bitcast_fusion.1 = bf16[8,2,64,2048]{3,2,0,1:T(8,128)(2,1)} fusion(bf16[1,2,704,2048]{3,2,1,0:T(8,128)(2,1)} %param.33, f32[2,8,64,704]{3,2,1,0:T(8,128)} %fusion.8, bf16[1,2,2048,704]{2,3,1,0:T(8,128)(2,1)} %param.31, bf16[8,2,64,2048]{3,2,1,0:T(8,128)(2,1)} %bitcast.283), kind=kOutput, calls=%fused_computation.31 | convolution fusion | flops 5912002560 | bytes 22806528 | tf_op jit(solution)/shard_map/jenf,efd->jend/dot_general | solution.py:145
  166.9 4.7 copy.29
  171.7 7.1 %all-to-all-start.1 = ((bf16[16,64,2048]{2,1,0:T(8,128)(2,1)}), bf16[16,64,2048]{2,1,0:T(8,128)(2,1)}, u32[]{:S(2)}, u32[]{:S(2)}) async-start(bf16[16,64,2048]{2,1,0:T(8,128)(2,1)} %bitcast.280), calls=%async_computation.1 | async-start | bytes 8388608 | tf_op jit(solution)/shard_map/all_to_all | solution.py:152
  181.0 88.2 %all-to-all-done.1 = bf16[16,64,2048]{2,1,0:T(8,128)(2,1)} async-done(((bf16[16,64,2048]{2,1,0:T(8,128)(2,1)}), bf16[16,64,2048]{2,1,0:T(8,128)(2,1)}, u32[]{:S(2)}, u32[]{:S(2)}) %all-to-all-start.1) | async-done | bytes 4194336 | tf_op jit(solution)/shard_map/all_to_all | solution.py:152
  269.2 9.8 %gather_fusion.1 = bf16[768,2048]{1,0:T(8,128)(2,1)} fusion(bf16[1024,2048]{1,0:T(8,128)(2,1)} %bitcast.32, s32[1024]{0:T(1024)S(1)} %pad_clamp_fusion.1), kind=kCustom, calls=%fused_computation.1 | custom fusion | bytes 6294528 | tf_op jit(solution)/shard_map/gather | solution.py:159
  279.0 6.6 %reshape.300 = f32[128,6,2048]{2,1,0:T(8,128)} reshape(bf16[768,2048]{1,0:T(8,128)(2,1)} %gather_fusion.1) | data formatting | bytes 9437184 | tf_op jit(solution)/shard_map/convert_element_type | solution.py:159
  285.6 6.7 %multiply_reduce_fusion.1 = f32[128,2048]{1,0:T(8,128)S(1)} fusion(f32[128,6,2048]{2,1,0:T(8,128)} %reshape.300, f32[128,6]{1,0:T(8,128)S(1)} %bitcast.287), kind=kLoop, calls=%fused_computation.9 | loop fusion | flops 2883584 | bytes 7343104 | tf_op jit(solution)/shard_map/reduce_sum | solution.py:163
  298.0 10.3 %collective-permute-done = bf16[128,2048]{1,0:T(8,128)(2,1)} collective-permute-done((bf16[128,2048]{1,0:T(8,128)(2,1)S(1)}, bf16[128,2048]{1,0:T(8,128)(2,1)}, u32[]{:S(2)}, u32[]{:S(2)}) %collective-permute-start) | collective-permute-done | bytes 524320 | tf_op jit(solution)/shard_map/ppermute | solution.py:16
  313.6 4.5 fusion.93
  318.1 6.8 %fusion.182 = (f32[128,8]{0,1:T(8,128)S(1)}, f32[128,8,896]{2,0,1:T(8,128)}) fusion(f32[128,8,896]{2,0,1:T(8,128)} %fusion.93, pred[128,896]{1,0:T(8,128)(4,1)S(1)} %copy-done.17), kind=kOutput, calls=%fused_computation.197 | output fusion | flops 6423423 | bytes 7458816 | tf_op jit(solution)/shard_map/sub | solution.py:37
  331.9 6.0 %gather_fusion.2 = bf16[1024,2048]{1,0:T(8,128)(2,1)} fusion(bf16[129,2048]{1,0:T(8,128)(2,1)S(1)} %concatenate.15, s32[1024]{0:T(1024)S(1)} %fusion.160), kind=kCustom, calls=%fused_computation.2 | custom fusion | bytes 8392704 | tf_op jit(solution)/shard_map/gather | solution.py:128
  337.9 98.6 %all_to_all.21 = bf16[16,64,2048]{2,1,0:T(8,128)(2,1)S(1)} all-to-all(bf16[16,64,2048]{2,1,0:T(8,128)(2,1)} %bitcast.279), channel_id=1, replica_groups=mesh['groups'=2,'expert'=8,'section'=2,'tensor'=1] {'expert'}, dimensions={0} | all-to-all | bytes 8388608 | tf_op jit(solution)/shard_map/all_to_all | solution.py:129
  438.5 7.8 %fusion.6 = f32[2,8,64,704]{3,2,1,0:T(8,128)} fusion(bf16[1,2,2048,704]{2,3,1,0:T(8,128)(2,1)} %param.32, bf16[8,2,64,2048]{3,2,1,0:T(8,128)(2,1)S(1)} %bitcast.284), kind=kOutput, calls=%fused_computation.14 | convolution fusion | flops 2952790016 | bytes 12845056 | tf_op jit(solution)/shard_map/jend,edf->jenf/dot_general | solution.py:138
  446.3 13.1 %convert_bitcast_fusion = bf16[8,2,64,2048]{3,2,0,1:T(8,128)(2,1)} fusion(bf16[1,2,704,2048]{3,2,1,0:T(8,128)(2,1)} %param.33, f32[2,8,64,704]{3,2,1,0:T(8,128)} %fusion.6, bf16[1,2,2048,704]{2,3,1,0:T(8,128)(2,1)} %param.31, bf16[8,2,64,2048]{3,2,1,0:T(8,128)(2,1)} %bitcast.285), kind=kOutput, calls=%fused_computation.30 | convolution fusion | flops 5912002560 | bytes 22806528 | tf_op jit(solution)/shard_map/jenf,efd->jend/dot_general | solution.py:145
  459.4 4.7 copy.37
  464.2 7.1 %all-to-all-start.3 = ((bf16[16,64,2048]{2,1,0:T(8,128)(2,1)}), bf16[16,64,2048]{2,1,0:T(8,128)(2,1)}, u32[]{:S(2)}, u32[]{:S(2)}) async-start(bf16[16,64,2048]{2,1,0:T(8,128)(2,1)} %bitcast.281), calls=%async_computation.3 | async-start | bytes 8388608 | tf_op jit(solution)/shard_map/all_to_all | solution.py:152
  471.4 90.3 %all-to-all-done.3 = bf16[16,64,2048]{2,1,0:T(8,128)(2,1)} async-done(((bf16[16,64,2048]{2,1,0:T(8,128)(2,1)}), bf16[16,64,2048]{2,1,0:T(8,128)(2,1)}, u32[]{:S(2)}, u32[]{:S(2)}) %all-to-all-start.3) | async-done | bytes 4194336 | tf_op jit(solution)/shard_map/all_to_all | solution.py:152
  561.7 9.8 %gather_fusion.3 = bf16[768,2048]{1,0:T(8,128)(2,1)} fusion(bf16[1024,2048]{1,0:T(8,128)(2,1)} %bitcast.52, s32[1024]{0:T(1024)S(1)} %pad_clamp_fusion), kind=kCustom, calls=%fused_computation.3 | custom fusion | bytes 6294528 | tf_op jit(solution)/shard_map/gather | solution.py:159
  571.6 6.6 %reshape.301 = f32[128,6,2048]{2,1,0:T(8,128)} reshape(bf16[768,2048]{1,0:T(8,128)(2,1)} %gather_fusion.3) | data formatting | bytes 9437184 | tf_op jit(solution)/shard_map/convert_element_type | solution.py:159
  578.1 6.8 %multiply_reduce_fusion = f32[128,2048]{1,0:T(8,128)S(1)} fusion(f32[128,6,2048]{2,1,0:T(8,128)} %reshape.301, f32[128,6]{1,0:T(8,128)S(1)} %bitcast.288), kind=kLoop, calls=%fused_computation.8 | loop fusion | flops 2883584 | bytes 7343104 | tf_op jit(solution)/shard_map/reduce_sum | solution.py:163
  (121 shorter events, 58.6 us)
Async XLA Ops:
  0.0 4.1 copy-start
  0.0 7.0 %copy-start.4 = (bf16[1,128,2048]{2,1,0:T(8,128)(2,1)S(1)}, bf16[1,128,2048]{2,1,0:T(8,128)(2,1)}, u32[]{:S(2)}) copy-start(bf16[1,128,2048]{2,1,0:T(8,128)(2,1)} %param.17) | copy-start | bytes 1572868
  0.0 7.0 %copy-start.18 = (f32[1,2048]{1,0:T(1,128)S(1)}, f32[1,2048]{1,0:T(1,128)}, u32[]{:S(2)}) copy-start(f32[1,2048]{1,0:T(1,128)} %param.23) | copy-start | bytes 24580
  4.1 5.9 %copy-start.15 = (bf16[2,1,1,768,512]{4,3,2,1,0:T(8,128)(2,1)S(1)}, bf16[2,1,1,768,512]{4,3,2,1,0:T(8,128)(2,1)}, u32[]{:S(2)}) copy-start(bf16[2,1,1,768,512]{4,3,2,1,0:T(8,128)(2,1)} %param.19) | copy-start | bytes 4718596
  7.0 4.2 copy-start.25
  10.0 5.7 copy-start.9
  20.2 6.8 %copy-start.12 = (bf16[768,512]{1,0:T(8,128)(2,1)S(1)}, bf16[768,512]{1,0:T(8,128)(2,1)}, u32[]{:S(2)}) copy-start(bf16[768,512]{1,0:T(8,128)(2,1)} %get-tuple-element.8) | copy-start | bytes 2359300
  31.0 5.2 copy-start.22
  31.0 9.1 %copy-start.19 = (f32[1,2048]{1,0:T(1,128)S(1)}, f32[1,2048]{1,0:T(1,128)}, u32[]{:S(2)}) copy-start(f32[1,2048]{1,0:T(1,128)} %param.30) | copy-start | bytes 24580
  34.1 6.0 %copy-start.2 = (f32[128,2048]{1,0:T(8,128)}, f32[128,2048]{1,0:T(8,128)S(1)}, u32[]{:S(2)}) copy-start(f32[128,2048]{1,0:T(8,128)S(1)} %get-tuple-element.24) | copy-start | bytes 3145732
  171.6 7.1 %copy-start.21 = (s32[1,1,128,6]{2,1,3,0:T(1,128)S(1)}, s32[1,1,128,6]{2,1,3,0:T(1,128)}, u32[]{:S(2)}) copy-start(s32[1,1,128,6]{2,1,3,0:T(1,128)} %get-tuple-element.11) | copy-start | bytes 9220
  171.7 7.5 %copy-start.24 = (f32[2,1,128,6]{2,1,3,0:T(1,128)S(1)}, f32[2,1,128,6]{2,1,3,0:T(1,128)}, u32[]{:S(2)}) copy-start(f32[2,1,128,6]{2,1,3,0:T(1,128)} %param.22) | copy-start | bytes 18436
  171.7 97.6 %all-to-all-start.1 = ((bf16[16,64,2048]{2,1,0:T(8,128)(2,1)}), bf16[16,64,2048]{2,1,0:T(8,128)(2,1)}, u32[]{:S(2)}, u32[]{:S(2)}) async-start(bf16[16,64,2048]{2,1,0:T(8,128)(2,1)} %bitcast.280), calls=%async_computation.1 | async-start | bytes 8388608 | tf_op jit(solution)/shard_map/all_to_all | solution.py:152
  285.6 6.7 %copy-start.3 = (f32[128,2048]{1,0:T(8,128)S(1)}, f32[128,2048]{1,0:T(8,128)}, u32[]{:S(2)}) copy-start(f32[128,2048]{1,0:T(8,128)} %copy-done.2) | copy-start | bytes 3145732
  285.6 8.4 %copy-start.20 = (s32[1,1,128,6]{2,1,3,0:T(1,128)S(1)}, s32[1,1,128,6]{2,1,3,0:T(1,128)}, u32[]{:S(2)}) copy-start(s32[1,1,128,6]{2,1,3,0:T(1,128)} %get-tuple-element.13) | copy-start | bytes 9220
  285.6 22.8 %copy-start.16 = (bf16[1,128,2048]{2,1,0:T(8,128)(2,1)S(1)}, bf16[1,128,2048]{2,1,0:T(8,128)(2,1)}, u32[]{:S(2)}) copy-start(bf16[1,128,2048]{2,1,0:T(8,128)(2,1)} %param.18) | copy-start | bytes 1572868
  292.5 17.2 %copy-start.13 = (bf16[128,2048]{1,0:T(8,128)(2,1)}, bf16[128,2048]{1,0:T(8,128)(2,1)S(1)}, u32[]{:S(2)}) copy-start(bf16[128,2048]{1,0:T(8,128)(2,1)S(1)} %add_convert_fusion.1) | copy-start | bytes 1572868
  292.5 15.9 %collective-permute-start = (bf16[128,2048]{1,0:T(8,128)(2,1)S(1)}, bf16[128,2048]{1,0:T(8,128)(2,1)}, u32[]{:S(2)}, u32[]{:S(2)}) collective-permute-start(bf16[128,2048]{1,0:T(8,128)(2,1)S(1)} %add_convert_fusion.1), channel_id=1, source_target_pairs={{0,1},{2,3},{4,5},{6,7},{8,9},{10,11},{12,13},{14,15},{16,17},{18,... | collective-permute-start | bytes 1572872 | tf_op jit(solution)/shard_map/ppermute | solution.py:16
  313.5 4.6 copy-start.17
  318.1 6.8 %copy-start.11 = (bf16[768,512]{1,0:T(8,128)(2,1)S(1)}, bf16[768,512]{1,0:T(8,128)(2,1)}, u32[]{:S(2)}) copy-start(bf16[768,512]{1,0:T(8,128)(2,1)} %get-tuple-element.7) | copy-start | bytes 2359300
  318.1 6.8 %copy-start.26 = (bf16[1,8,512,128]{3,2,1,0:T(8,128)(2,1)S(1)}, bf16[1,8,512,128]{3,2,1,0:T(8,128)(2,1)}, u32[]{:S(2)}) copy-start(bf16[1,8,512,128]{3,2,1,0:T(8,128)(2,1)} %param.26) | copy-start | bytes 3145732
  464.2 97.5 %all-to-all-start.3 = ((bf16[16,64,2048]{2,1,0:T(8,128)(2,1)}), bf16[16,64,2048]{2,1,0:T(8,128)(2,1)}, u32[]{:S(2)}, u32[]{:S(2)}) async-start(bf16[16,64,2048]{2,1,0:T(8,128)(2,1)} %bitcast.281), calls=%async_computation.3 | async-start | bytes 8388608 | tf_op jit(solution)/shard_map/all_to_all | solution.py:152
  578.1 6.9 %copy-start.14 = (bf16[128,2048]{1,0:T(8,128)(2,1)S(1)}, bf16[128,2048]{1,0:T(8,128)(2,1)}, u32[]{:S(2)}) copy-start(bf16[128,2048]{1,0:T(8,128)(2,1)} %copy-done.13) | copy-start | bytes 1572868
  578.1 8.0 %copy-start.1 = (bf16[1,2048,512]{2,1,0:T(8,128)(2,1)S(1)}, bf16[1,2048,512]{2,1,0:T(8,128)(2,1)}, u32[]{:S(2)}) copy-start(bf16[1,2048,512]{2,1,0:T(8,128)(2,1)} %param.28) | copy-start | bytes 6291460
  (6 other events, 19.2 us)
where the time goes:
time: 598 us; the launch traced here: 587 us
  blocking collectives  196 us (33%)
  waiting for transfers between devices  189 us (32%)
  matrix products  73.8 us (12%)
  local copies, waits for them, and re-layouts  69.4 us (12%)
  other arithmetic  41.9 us (7%)
  starting transfers between devices  15.5 us (3%)
    all_to_all x2, blocking collectives, shards(): lax.all_to_all(outbox, 'expert', split_axis=0, concat_axis=0, tiled=True)  196 us
    all_to_all x2, waiting for transfers between devices, shards(): lax.all_to_all(partial_value, 'expert', split_axis=0, concat_axis=0, tile...  179 us
    dot_general x2, matrix products, shards(): jnp.einsum('jenf,efd->jend', hidden, specialist_contract_factor[0], prefe...  26.2 us
    gather x2, local copies, waits for them, and re-layouts, shards(): expert_out.reshape(EXPERTS * CAP, inner_feature_midcount)[target]  19.6 us
    dot_general x2, matrix products, shards(): jnp.einsum('jend,edf->jenf', grouped, specialist_widen_factor[0], preferr...  15.7 us
    all_to_all x2, starting transfers between devices, shards(): lax.all_to_all(partial_value, 'expert', split_axis=0, concat_axis=0, tile...  14.2 us
    sub x2, other arithmetic, attend(): expd = jnp.where(visible[:, None, :], jnp.exp(scores - row_max), 0.0)  13.6 us
    reduce_sum x2, other arithmetic, shards(): jnp.sum(picked * chooser_mixing_share[step_index, 0][:, :, None], axis=1)  13.5 us
  transfers between devices with their start and end apart: 3, of which 3 were waited for; matrix products, arithmetic and copies ran while one was open for 1% of the time, Pallas kernels for 0%

commit v1 on v0

--- a/solution.py
+++ b/solution.py
@@ -3,8 +3,8 @@
 from jax import lax
 from jax.sharding import PartitionSpec as P
 
-EXPERTS = 16
 CAP = 64
+RETURN_CHUNKS = 2
 
 
 epsilon = 1e-06
@@ -72,6 +72,36 @@
     top_count = picked_specialists.shape[3]
     expert_local = specialist_switch_factor.shape[1]
     score_scale = head_size ** (-0.5)
+    expert_ids = lax.broadcasted_iota(jnp.int32, (1, 1, 1, expert_local * sources), 3)
+    shares_dense = jnp.sum(
+        jnp.where(
+            picked_specialists[:, 0][..., None] == expert_ids,
+            chooser_mixing_share[:, 0][..., None],
+            0.0,
+        ),
+        axis=2,
+    )
+    shares_all = lax.all_gather(
+        jnp.swapaxes(shares_dense, 1, 2), "expert", axis=1, tiled=False
+    )
+    mine = lax.dynamic_slice_in_dim(
+        shares_all, lax.axis_index("expert") * expert_local, expert_local, axis=2
+    )
+    chosen = mine > 0.0
+    earlier_or_same = (
+        lax.broadcasted_iota(jnp.int32, (piece_list, piece_list), 0)
+        <= lax.broadcasted_iota(jnp.int32, (piece_list, piece_list), 1)
+    ).astype(jnp.bfloat16)
+    rank = jnp.einsum(
+        "tjer,rq->tjeq",
+        chosen.astype(jnp.bfloat16),
+        earlier_or_same,
+        preferred_element_type=jnp.float32,
+    ).astype(jnp.int32)
+    slots = lax.broadcasted_iota(jnp.int32, (1, 1, 1, CAP, 1), 3) + 1
+    at_slot = (rank[..., None, :] == slots) & chosen[..., None, :]
+    placed = at_slot.astype(jnp.bfloat16)
+    slot_share = jnp.sum(jnp.where(at_slot, mine[..., None, :], 0.0), axis=-1)
     outputs = []
     present_carry = opening_residual[0]
     section_out = present_carry
@@ -114,53 +144,53 @@
             * lax.rsqrt(squares / full_width + epsilon)[:, None]
             * specialist_scale_factor[0]
         ).astype(jnp.bfloat16)
-        choices = picked_specialists[step_index, 0].reshape(-1)
-        onehot = (choices[:, None] == lax.broadcasted_iota(jnp.int32, (1, EXPERTS), 1)).astype(
-            jnp.int32
-        )
-        earlier = jnp.cumsum(onehot, axis=0) - onehot
-        slot_index = jnp.sum(earlier * onehot, axis=1)
-        target = choices * CAP + slot_index
-        owner_row = lax.broadcasted_iota(jnp.int32, (piece_list, top_count), 0).reshape(-1)
-        source = jnp.full((EXPERTS * CAP,), piece_list, jnp.int32).at[target].set(owner_row)
         whole_rows = lax.all_gather(moe_input, "tensor", axis=1, tiled=True)
-        padded = jnp.concatenate([whole_rows, jnp.zeros((1, full_width), jnp.bfloat16)], axis=0)
-        outbox = padded[source].reshape(EXPERTS, CAP, full_width)
-        received = lax.all_to_all(outbox, "expert", split_axis=0, concat_axis=0, tiled=True)
-        item_count = received.shape[1]
-        grouped = received.reshape(sources, expert_local, item_count, full_width)
-        serve_gate_values = jnp.einsum(
-            "jend,edf->jenf",
-            grouped,
-            specialist_switch_factor[0],
-            preferred_element_type=jnp.float32,
-        )
-        serve_up_values = jnp.einsum(
-            "jend,edf->jenf",
-            grouped,
-            specialist_widen_factor[0],
-            preferred_element_type=jnp.float32,
-        )
-        hidden = (jax.nn.silu(serve_gate_values) * serve_up_values).astype(jnp.bfloat16)
-        partial_value = jnp.einsum(
-            "jenf,efd->jend",
-            hidden,
-            specialist_contract_factor[0],
-            preferred_element_type=jnp.float32,
-        ).astype(jnp.bfloat16)
-        partial_value = partial_value.reshape(sources * expert_local, item_count, full_width)
-        returned = lax.all_to_all(partial_value, "expert", split_axis=0, concat_axis=0, tiled=True)
-        expert_out = lax.psum_scatter(
-            returned.astype(jnp.float32).astype(jnp.bfloat16),
-            "tensor",
-            scatter_dimension=2,
-            tiled=True,
-        )
-        picked = expert_out.reshape(EXPERTS * CAP, inner_feature_midcount)[target].astype(
+        place = placed[step_index]
+        share = slot_share[step_index]
+        all_rows = lax.all_gather(whole_rows, "expert", axis=0, tiled=True)
+        all_rows = all_rows.reshape(sources, piece_list, full_width)
+        hidden_list = []
+        for e in range(expert_local):
+            rows_in = jnp.einsum(
+                "jsr,jrd->jsd", place[:, e], all_rows, preferred_element_type=jnp.float32
+            ).astype(jnp.bfloat16)
+            rows_in = rows_in.reshape(sources * CAP, full_width)
+            gate_values = jnp.dot(
+                rows_in, specialist_switch_factor[0, e], preferred_element_type=jnp.float32
+            )
+            up_values = jnp.dot(
+                rows_in, specialist_widen_factor[0, e], preferred_element_type=jnp.float32
+            )
+            hidden_list.append(
+                (jax.nn.silu(gate_values) * up_values * share[:, e].reshape(-1, 1)).astype(
+                    jnp.bfloat16
+                )
+            )
+        chunk = full_width // RETURN_CHUNKS
+        routed_list = []
+        for c in range(RETURN_CHUNKS):
+            total = None
+            for e in range(expert_local):
+                down = jnp.dot(
+                    hidden_list[e],
+                    specialist_contract_factor[0, e][:, c * chunk : (c + 1) * chunk],
+                    preferred_element_type=jnp.float32,
+                ).astype(jnp.bfloat16)
+                term = jnp.einsum(
+                    "jsr,jsd->jrd",
+                    place[:, e],
+                    down.reshape(sources, CAP, chunk),
+                    preferred_element_type=jnp.float32,
+                )
+                total = term if total is None else total + term
+            total = total.astype(jnp.bfloat16).reshape(sources * piece_list, chunk)
+            routed_list.append(
+                lax.psum_scatter(total, "expert", scatter_dimension=0, tiled=True)
+            )
+        routed = jnp.concatenate(routed_list, axis=1)
+        routed = lax.psum_scatter(routed, "tensor", scatter_dimension=1, tiled=True).astype(
             jnp.float32
         )
-        picked = picked.reshape(piece_list, top_count, inner_feature_midcount)
-        routed = jnp.sum(picked * chooser_mixing_share[step_index, 0][:, :, None], axis=1)
         section_out = (residual + routed).astype(jnp.bfloat16)
         outputs.append(section_out)
     return jnp.stack(outputs)[:, None]

time: 598 us -> 374 us (0.63)
  the two profiles are of different devices: /device:TPU:10 before, /device:TPU:0 now
where the time goes in v1:
time: 374 us; the launch traced here: 369 us
  waiting for transfers between devices  213 us (57%)
  matrix products  81 us (22%)
  other arithmetic  29.1 us (8%)
  blocking collectives  16 us (4%)
  between operations  14.8 us (4%)
  local copies, waits for them, and re-layouts  10.7 us (3%)
  starting transfers between devices  4.3 us (1%)
    reduce_scatter x4, waiting for transfers between devices, shards(): lax.psum_scatter(total, 'expert', scatter_dimension=0, tiled=True)  131 us
    all_gather x2, waiting for transfers between devices, shards(): all_rows = lax.all_gather(whole_rows, 'expert', axis=0, tiled=True)  73.4 us
    all_gather x1, blocking collectives, shards(): lax.all_gather(jnp.swapaxes(shares_dense, 1, 2), 'expert', axis=1, tiled=...  16 us
    sub x2, other arithmetic, attend(): expd = jnp.where(visible[:, None, :], jnp.exp(scores - row_max), 0.0)  13.5 us
    dot_general x8, matrix products, shards(): jnp.einsum('jsr,jsd->jrd', place[:, e], down.reshape(sources, CAP, chunk)...  11.9 us
    dot_general x8, matrix products, shards(): jnp.dot(hidden_list[e], specialist_contract_factor[0, e][:, c * chunk:(c...  11.2 us
    dot_general x4, matrix products, shards(): jnp.dot(rows_in, specialist_switch_factor[0, e], preferred_element_type=j...  10.9 us
    dot_general x2, matrix products, attend(): jnp.einsum('thl,kl->thk', q_lat, key_rows, preferred_element_type=jnp.flo...  9.03 us
  transfers between devices with their start and end apart: 7, of which 7 were waited for; matrix products, arithmetic and copies ran while one was open for 6% of the time, Pallas kernels for 0%

profile of v1, /device:TPU:0, one launch (start us, length us, event | category | flops | bytes accessed | tf_op | source)
XLA Modules:
  0.0 368.7 jit_solution(13593333180121278280)
XLA Ops:
  11.3 3.0 fusion.130
  20.1 4.5 %fusion.105 = f32[128,8,896]{2,0,1:T(8,128)} fusion(bf16[1,8,128,512]{3,2,1,0:T(8,128)(2,1)S(1)} %copy-done.7, bf16[128,512]{1,0:T(8,128)(2,1)S(1)} %multiply_convert_fusion.3, bf16[768,512]{1,0:T(8,128)(2,1)} %get-tuple-element.10, bf16[16,8,8,128]{3,2,1,0:T(8,128)(2,1)S(1)} %fusion.130), kind=kOutput, calls=%fused_computation.97 | convolution fusion | flops 1076101120 | bytes 5898240 | tf_op jit(solution)/shard_map/thl,kl->thk/dot_general | solution.py:30
  24.6 6.7 %fusion.191 = (f32[128,8]{0,1:T(8,128)S(1)}, f32[128,8,896]{2,0,1:T(8,128)}) fusion(f32[128,8,896]{2,0,1:T(8,128)} %fusion.105, pred[128,896]{1,0:T(8,128)(4,1)} %get-tuple-element.20), kind=kOutput, calls=%fused_computation.204 | output fusion | flops 6423423 | bytes 7458816 | tf_op jit(solution)/shard_map/sub | solution.py:37
  31.3 3.9 %fusion.126 = bf16[8,128,128]{1,2,0:T(8,128)(2,1)S(1)} fusion(f32[128,8,896]{2,0,1:T(8,128)} %get-tuple-element.26, f32[128,8]{0,1:T(8,128)S(1)} %get-tuple-element.25, bf16[1,8,512,128]{3,2,1,0:T(8,128)(2,1)} %param.26, bf16[128,512]{1,0:T(8,128)(2,1)S(1)} %multiply_convert_fusion.3, bf16[768,512]{1,0:T(8,128)(2,1)S(1)} %copy-done.10), kind=kOutput, calls=%fused_computation.116 | convolution fusion | flops 1078067200 | bytes 5902336 | tf_op jit(solution)/shard_map/thl,hld->thd/dot_general | solution.py:133
  35.3 3.1 multiply_reduce_fusion.1
  39.6 16.0 %all-gather = f32[2,128,128]{2,1,0:T(8,128)S(1)} all-gather(f32[2,16,128]{2,1,0:T(8,128)S(1)} %bitcast.305), channel_id=2, replica_groups=mesh['groups'=2,'expert'=8,'section'=2,'tensor'=1] {'expert'}, dimensions={1}, use_global_device_ids=true | all-gather | bytes 147456 | tf_op jit(solution)/shard_map/all_gather | solution.py:84
  57.3 6.3 %slice_bitcast_fusion = (bf16[704,2048]{1,0:T(8,128)(2,1)}, bf16[704,2048]{1,0:T(8,128)(2,1)}) fusion(bf16[1,2,704,2048]{3,2,1,0:T(8,128)(2,1)} %param.33), kind=kLoop, calls=%fused_computation.40 | loop fusion | bytes 11534336 | tf_op jit(solution)/shard_map/squeeze | solution.py:176
  63.7 25.7 %all-gather.4.cloned.1.call-done = bf16[1024,2048]{1,0:T(8,128)(2,1)} async-done(((bf16[128,2048]{1,0:T(8,128)(2,1)}), bf16[1024,2048]{1,0:T(8,128)(2,1)}) %all-gather.4.cloned.1.call-update) | async-done | bytes 4194320 | tf_op jit(solution)/shard_map/all_gather | solution.py:150
  89.4 3.0 convolution_convert_fusion.2
  93.6 3.9 %fusion.16 = f32[512,704]{0,1:T(8,128)S(1)} fusion(bf16[512,2048]{1,0:T(8,128)(2,1)S(1)} %bitcast.286, bf16[1,2,2048,704]{2,3,1,0:T(8,128)(2,1)} %param.31), kind=kOutput, calls=%fused_computation.30 | convolution fusion | flops 1476395008 | bytes 6422528 | tf_op jit(solution)/shard_map/dot_general | solution.py:158
  115.0 28.7 %reduce-scatter.5.cloned.1.call-done = bf16[128,1024]{1,0:T(8,128)(2,1)} async-done(((bf16[1024,1024]{1,0:T(8,128)(2,1)}), bf16[128,1024]{1,0:T(8,128)(2,1)}) %reduce-scatter.5.cloned.1.call-update) | async-done | bytes 262160 | tf_op jit(solution)/shard_map/reduce_scatter | solution.py:188
  143.7 36.8 %reduce-scatter.7.cloned.1.call-done = bf16[128,1024]{1,0:T(8,128)(2,1)} async-done(((bf16[1024,1024]{1,0:T(8,128)(2,1)}), bf16[128,1024]{1,0:T(8,128)(2,1)}) %reduce-scatter.7.cloned.1.call-update) | async-done | bytes 262160 | tf_op jit(solution)/shard_map/reduce_scatter | solution.py:188
  182.5 3.5 collective-permute-start
  186.1 8.7 %collective-permute-done = bf16[128,2048]{1,0:T(8,128)(2,1)S(1)} collective-permute-done((bf16[128,2048]{1,0:T(8,128)(2,1)}, bf16[128,2048]{1,0:T(8,128)(2,1)S(1)}, u32[]{:S(2)}, u32[]{:S(2)}) %collective-permute-start) | collective-permute-done | bytes 524320 | tf_op jit(solution)/shard_map/ppermute | solution.py:16
  196.1 3.2 fusion.127
  200.5 4.5 %fusion.107 = f32[128,8,896]{2,0,1:T(8,128)} fusion(bf16[1,8,128,512]{3,2,1,0:T(8,128)(2,1)S(1)} %copy-done.8, bf16[128,512]{1,0:T(8,128)(2,1)S(1)} %multiply_convert_fusion.2, bf16[768,512]{1,0:T(8,128)(2,1)} %get-tuple-element.9, bf16[16,8,8,128]{3,2,1,0:T(8,128)(2,1)S(1)} %fusion.127), kind=kOutput, calls=%fused_computation.99 | convolution fusion | flops 1076101120 | bytes 5898240 | tf_op jit(solution)/shard_map/thl,kl->thk/dot_general | solution.py:30
  205.0 6.7 %fusion.192 = (f32[128,8]{0,1:T(8,128)S(1)}, f32[128,8,896]{2,0,1:T(8,128)}) fusion(f32[128,8,896]{2,0,1:T(8,128)} %fusion.107, pred[128,896]{1,0:T(8,128)(4,1)S(1)} %copy-done.18), kind=kOutput, calls=%fused_computation.205 | output fusion | flops 6423423 | bytes 7458816 | tf_op jit(solution)/shard_map/sub | solution.py:37
  211.8 3.7 %fusion.125 = bf16[8,128,128]{1,2,0:T(8,128)(2,1)S(1)} fusion(f32[128,8,896]{2,0,1:T(8,128)} %get-tuple-element.32, f32[128,8]{0,1:T(8,128)S(1)} %get-tuple-element.31, bf16[1,8,512,128]{3,2,1,0:T(8,128)(2,1)S(1)} %copy-done.28, bf16[128,512]{1,0:T(8,128)(2,1)S(1)} %multiply_convert_fusion.2, bf16[768,512]{1,0:T(8,128)(2,1)S(1)} %copy-done.9), kind=kOutput, calls=%fused_computation.115 | convolution fusion | flops 1078067200 | bytes 5902336 | tf_op jit(solution)/shard_map/thl,hld->thd/dot_general | solution.py:133
  215.5 3.0 multiply_reduce_fusion
  220.0 47.7 %all-gather.6.cloned.1.call-done = bf16[1024,2048]{1,0:T(8,128)(2,1)} async-done(((bf16[128,2048]{1,0:T(8,128)(2,1)}), bf16[1024,2048]{1,0:T(8,128)(2,1)}) %all-gather.6.cloned.1.call-update) | async-done | bytes 4194320 | tf_op jit(solution)/shard_map/all_gather | solution.py:150
  267.7 3.0 convolution_convert_fusion
  271.8 3.6 fusion.14
  293.1 28.2 %reduce-scatter.9.cloned.1.call-done = bf16[128,1024]{1,0:T(8,128)(2,1)} async-done(((bf16[1024,1024]{1,0:T(8,128)(2,1)}), bf16[128,1024]{1,0:T(8,128)(2,1)}) %reduce-scatter.9.cloned.1.call-update) | async-done | bytes 262160 | tf_op jit(solution)/shard_map/reduce_scatter | solution.py:188
  321.3 36.8 %reduce-scatter.11.cloned.1.call-done = bf16[128,1024]{1,0:T(8,128)(2,1)} async-done(((bf16[1024,1024]{1,0:T(8,128)(2,1)}), bf16[128,1024]{1,0:T(8,128)(2,1)}) %reduce-scatter.11.cloned.1.call-update) | async-done | bytes 262160 | tf_op jit(solution)/shard_map/reduce_scatter | solution.py:188
  (170 shorter events, 59.3 us)
Async XLA Ops:
  6.5 4.8 %copy-start.4 = (bf16[1,128,2048]{2,1,0:T(8,128)(2,1)S(1)}, bf16[1,128,2048]{2,1,0:T(8,128)(2,1)}, u32[]{:S(2)}) copy-start(bf16[1,128,2048]{2,1,0:T(8,128)(2,1)} %param.17) | copy-start | bytes 1572868
  6.5 4.8 %copy-start.19 = (f32[1,2048]{1,0:T(1,128)S(1)}, f32[1,2048]{1,0:T(1,128)}, u32[]{:S(2)}) copy-start(f32[1,2048]{1,0:T(1,128)} %param.23) | copy-start | bytes 24580
  6.5 82.8 %all-gather.4.cloned.1.call-start = ((), (), s32[]{:S(2)}) async-start(), calls=%async_computation.4 | async-start | bytes 4718592 | tf_op jit(solution)/shard_map/all_gather | solution.py:150
  11.3 4.3 %copy-start.27 = (s32[3,1]{0,1:T(1,128)S(1)}, s32[3,1]{0,1:T(1,128)}, u32[]{:S(2)}) copy-start(s32[3,1]{0,1:T(1,128)} %param.20) | copy-start | bytes 40
  11.3 6.1 %copy-start.23 = (f32[1,512]{1,0:T(1,128)S(1)}, f32[1,512]{1,0:T(1,128)}, u32[]{:S(2)}) copy-start(f32[1,512]{1,0:T(1,128)} %param.29) | copy-start | bytes 6148
  14.3 5.7 %copy-start.7 = (bf16[1,8,128,512]{3,2,1,0:T(8,128)(2,1)S(1)}, bf16[1,8,128,512]{3,2,1,0:T(8,128)(2,1)}, u32[]{:S(2)}) copy-start(bf16[1,8,128,512]{3,2,1,0:T(8,128)(2,1)} %param.25) | copy-start | bytes 3145732
  24.6 6.7 %copy-start.10 = (bf16[768,512]{1,0:T(8,128)(2,1)S(1)}, bf16[768,512]{1,0:T(8,128)(2,1)}, u32[]{:S(2)}) copy-start(bf16[768,512]{1,0:T(8,128)(2,1)} %get-tuple-element.10) | copy-start | bytes 2359300
  39.5 104.3 %reduce-scatter.5.cloned.1.call-start = ((), (), s32[]{:S(2)}) async-start(), calls=%async_computation.5 | async-start | bytes 2359296 | tf_op jit(solution)/shard_map/reduce_scatter | solution.py:188
  92.8 4.6 %slice-start = ((s8[5767168]{0:T(1024)(128)(4,1)}), s8[4194304]{0:T(1024)(128)(4,1)S(1)}, s32[]{:S(2)}) async-start(s8[5767168]{0:T(1024)(128)(4,1)} %bitcast.316), calls=%async_computation.10 | async-start | bytes 8388608
  93.6 5.6 %slice-start.4 = ((s8[5767168]{0:T(1024)(128)(4,1)}), s8[4194304]{0:T(1024)(128)(4,1)S(1)}, s32[]{:S(2)}) async-start(s8[5767168]{0:T(1024)(128)(4,1)} %bitcast.320), calls=%async_computation.14 | async-start | bytes 8388608
  108.2 72.3 %reduce-scatter.7.cloned.1.call-start = ((), (), s32[]{:S(2)}) async-start(), calls=%async_computation.6 | async-start | bytes 2359296 | tf_op jit(solution)/shard_map/reduce_scatter | solution.py:188
  115.0 152.7 %all-gather.6.cloned.1.call-start = ((), (), s32[]{:S(2)}) async-start(), calls=%async_computation.7 | async-start | bytes 4718592 | tf_op jit(solution)/shard_map/all_gather | solution.py:150
  182.5 12.3 %collective-permute-start = (bf16[128,2048]{1,0:T(8,128)(2,1)}, bf16[128,2048]{1,0:T(8,128)(2,1)S(1)}, u32[]{:S(2)}, u32[]{:S(2)}) collective-permute-start(bf16[128,2048]{1,0:T(8,128)(2,1)} %add_convert_fusion.5), channel_id=1, source_target_pairs={{0,1},{2,3},{4,5},{6,7},{8,9},{10,11},{12,13},{14,15},{16,17},{18,... | collective-permute-start | bytes 1572872 | tf_op jit(solution)/shard_map/ppermute | solution.py:16
  200.5 4.5 %copy-start.18 = (pred[128,896]{1,0:T(8,128)(4,1)S(1)}, pred[128,896]{1,0:T(8,128)(4,1)}, u32[]{:S(2)}) copy-start(pred[128,896]{1,0:T(8,128)(4,1)} %get-tuple-element.19) | copy-start | bytes 344068
  205.0 6.8 %copy-start.9 = (bf16[768,512]{1,0:T(8,128)(2,1)S(1)}, bf16[768,512]{1,0:T(8,128)(2,1)}, u32[]{:S(2)}) copy-start(bf16[768,512]{1,0:T(8,128)(2,1)} %get-tuple-element.9) | copy-start | bytes 2359300
  205.0 6.8 %copy-start.28 = (bf16[1,8,512,128]{3,2,1,0:T(8,128)(2,1)S(1)}, bf16[1,8,512,128]{3,2,1,0:T(8,128)(2,1)}, u32[]{:S(2)}) copy-start(bf16[1,8,512,128]{3,2,1,0:T(8,128)(2,1)} %param.26) | copy-start | bytes 3145732
  215.5 4.3 %copy-start.22 = (f32[8,1,64]{2,0,1:T(8,128)S(1)}, f32[8,1,64]{2,0,1:T(8,128)}, u32[]{:S(2)}) copy-start(f32[8,1,64]{2,0,1:T(8,128)} %get-tuple-element.15) | copy-start | bytes 6148
  215.5 4.4 %copy-start.21 = (f32[8,1,64]{2,0,1:T(8,128)S(1)}, f32[8,1,64]{2,0,1:T(8,128)}, u32[]{:S(2)}) copy-start(f32[8,1,64]{2,0,1:T(8,128)} %get-tuple-element.16) | copy-start | bytes 6148
  219.5 101.8 %reduce-scatter.9.cloned.1.call-start = ((), (), s32[]{:S(2)}) async-start(), calls=%async_computation.8 | async-start | bytes 2359296 | tf_op jit(solution)/shard_map/reduce_scatter | solution.py:188
  267.7 7.8 %slice-start.6 = ((s8[5767168]{0:T(1024)(128)(4,1)}), s8[4194304]{0:T(1024)(128)(4,1)S(1)}, s32[]{:S(2)}) async-start(s8[5767168]{0:T(1024)(128)(4,1)} %bitcast.322), calls=%async_computation.16 | async-start | bytes 8388608
  271.1 4.4 %slice-start.7 = ((s8[5767168]{0:T(1024)(128)(4,1)}), s8[1572864]{0:T(1024)(128)(4,1)S(1)}, s32[]{:S(2)}) async-start(s8[5767168]{0:T(1024)(128)(4,1)} %bitcast.322), calls=%async_computation.17 | async-start | bytes 3145728
  271.8 6.6 %slice-start.2 = ((s8[5767168]{0:T(1024)(128)(4,1)}), s8[4194304]{0:T(1024)(128)(4,1)S(1)}, s32[]{:S(2)}) async-start(s8[5767168]{0:T(1024)(128)(4,1)} %bitcast.318), calls=%async_computation.12 | async-start | bytes 8388608
  286.2 71.9 %reduce-scatter.11.cloned.1.call-start = ((), (), s32[]{:S(2)}) async-start(), calls=%async_computation.9 | async-start | bytes 2359296 | tf_op jit(solution)/shard_map/reduce_scatter | solution.py:188
  293.1 68.3 %copy-start.1 = (bf16[1,2048,512]{2,1,0:T(8,128)(2,1)S(1)}, bf16[1,2048,512]{2,1,0:T(8,128)(2,1)}, u32[]{:S(2)}) copy-start(bf16[1,2048,512]{2,1,0:T(8,128)(2,1)} %param.28) | copy-start | bytes 6291460
  (27 other events, 70.2 us)
Sparse Core Ops, SparseCore 0:
  39.6 49.7 all-gather.3
  108.4 35.3 reduce-scatter.4
  146.0 34.5 reduce-scatter.6
  219.7 47.9 all-gather.5
  286.4 34.8 reduce-scatter.8
  323.4 34.6 reduce-scatter.10

commit v2 on v1

--- a/solution.py
+++ b/solution.py
@@ -1,13 +1,281 @@
 import jax
 import jax.numpy as jnp
 from jax import lax
+from jax.experimental import pallas as pl
+from jax.experimental.pallas import tpu as pltpu
 from jax.sharding import PartitionSpec as P
 
 CAP = 64
-RETURN_CHUNKS = 2
+RETURN_CHUNKS = 1
 
 
 epsilon = 1e-06
+
+
+MESH = pl.DeviceIdType.MESH
+PIECES = 2
+
+
+def place_on_line():
+    count = lax.axis_size("expert")
+    pair = 2 if count % 2 == 0 else 1
+    mine = lax.axis_index("expert")
+    return count // pair, pair, mine, mine // pair, lax.rem(mine, pair)
+
+
+def greet(chips, pair, mine, spot, side):
+    barrier = pltpu.get_barrier_semaphore()
+
+    def hello(other):
+        pl.semaphore_signal(barrier, inc=1, device_id={"expert": other}, device_id_type=MESH)
+
+    @pl.when(spot > 0)
+    def _():
+        hello(mine - pair)
+
+    @pl.when(spot < chips - 1)
+    def _():
+        hello(mine + pair)
+
+    if pair == 2:
+        hello(mine + 1 - 2 * side)
+    inner = (spot > 0) & (spot < chips - 1)
+
+    @pl.when(inner)
+    def _():
+        pl.semaphore_wait(barrier, pair + 1)
+
+    @pl.when(jnp.logical_not(inner))
+    def _():
+        pl.semaphore_wait(barrier, pair)
+
+
+def remote(src, dst, send, recv, other):
+    return pltpu.make_async_remote_copy(
+        src_ref=src,
+        dst_ref=dst,
+        send_sem=send,
+        recv_sem=recv,
+        device_id={"expert": other},
+        device_id_type=MESH,
+    )
+
+
+def spread_kernel(own_ref, all_ref, own_sem, line_send, line_recv, side_send, side_recv):
+    chips, pair, mine, spot, side = place_on_line()
+    step = own_ref.shape[0] // PIECES
+    sibling = mine + 1 - 2 * side
+
+    def rows(block, core, piece):
+        return all_ref.at[block, core, pl.ds(piece * step, step)]
+
+    def line_copy(block, piece, way):
+        source = own_ref.at[pl.ds(piece * step, step)] if block is None else rows(block, side, piece)
+        where = spot if block is None else block
+        direction = 0 if way > 0 else 1
+        return remote(
+            source,
+            rows(where, side, piece),
+            line_send.at[direction, where, piece],
+            line_recv.at[where, piece],
+            mine + way * pair,
+        )
+
+    def side_copy(block, piece):
+        source = own_ref.at[pl.ds(piece * step, step)] if block is None else rows(block, side, piece)
+        where = spot if block is None else block
+        return remote(
+            source,
+            rows(where, side, piece),
+            side_send.at[where, piece],
+            side_recv.at[where, piece],
+            sibling,
+        )
+
+    def onward(block, piece, way, act):
+        @pl.when((spot < chips - 1) if way > 0 else (spot > 0))
+        def _():
+            act(line_copy(block, piece, way))
+
+    greet(chips, pair, mine, spot, side)
+    for piece in range(PIECES):
+        for way in (1, -1):
+            onward(None, piece, way, lambda copy: copy.start())
+    for piece in range(PIECES):
+        if pair == 2:
+            side_copy(None, piece).start()
+    keep = pltpu.make_async_copy(own_ref, all_ref.at[spot, side], own_sem)
+    keep.start()
+    for far in range(1, chips):
+        for piece in range(PIECES):
+            for way in (1, -1):
+                block = spot - way * far
+
+                @pl.when((block >= 0) if way > 0 else (block < chips))
+                def _():
+                    line_copy(block, piece, way).wait_recv()
+                    onward(block, piece, way, lambda copy: copy.start())
+                    if pair == 2:
+                        side_copy(block, piece).start()
+
+    keep.wait()
+    for piece in range(PIECES):
+        for way in (1, -1):
+            onward(None, piece, way, lambda copy: copy.wait_send())
+        if pair == 2:
+            side_copy(None, piece).wait()
+    for far in range(1, chips):
+        for piece in range(PIECES):
+            for way in (1, -1):
+                block = spot - way * far
+
+                @pl.when((block >= 0) if way > 0 else (block < chips))
+                def _():
+                    onward(block, piece, way, lambda copy: copy.wait_send())
+                    if pair == 2:
+                        side_copy(block, piece).wait()
+
+
+def spread(own):
+    count = lax.axis_size("expert")
+    pair = 2 if count % 2 == 0 else 1
+    chips = count // pair
+    result = pl.pallas_call(
+        spread_kernel,
+        out_shape=jax.ShapeDtypeStruct((chips, pair) + own.shape, own.dtype),
+        in_specs=[pl.BlockSpec(memory_space=pltpu.VMEM)],
+        out_specs=pl.BlockSpec(memory_space=pltpu.VMEM),
+        scratch_shapes=[
+            pltpu.SemaphoreType.DMA,
+            pltpu.SemaphoreType.DMA((2, chips, PIECES)),
+            pltpu.SemaphoreType.DMA((chips, PIECES)),
+            pltpu.SemaphoreType.DMA((chips, PIECES)),
+            pltpu.SemaphoreType.DMA((chips, PIECES)),
+        ],
+        compiler_params=pltpu.CompilerParams(collective_id=0, has_side_effects=True),
+    )(own)
+    return result.reshape((count,) + own.shape)
+
+
+def gather_sum_kernel(
+    part_ref, sum_ref, side_in, total, line_in, side_send, side_recv, line_send, line_recv
+):
+    chips, pair, mine, spot, side = place_on_line()
+    height = part_ref.shape[2]
+    step = height // PIECES
+    sibling = mine + 1 - 2 * side
+
+    def span(piece):
+        return pl.ds(piece * step, step)
+
+    def side_copy(block, piece):
+        return remote(
+            part_ref.at[block, 1 - side, span(piece)],
+            side_in.at[block, span(piece)],
+            side_send.at[block, piece],
+            side_recv.at[block, piece],
+            sibling,
+        )
+
+    def line_copy(block, piece, way):
+        direction = 0 if way > 0 else 1
+        return remote(
+            total.at[block, span(piece)],
+            line_in.at[direction, block, span(piece)],
+            line_send.at[block, piece],
+            line_recv.at[direction, block, piece],
+            mine + way * pair,
+        )
+
+    def wide(value):
+        return value.astype(jnp.float32)
+
+    def chip_sum(block, piece):
+        value = wide(part_ref[block, side, span(piece)])
+        if pair == 2:
+            side_copy(block, piece).wait_recv()
+            value = value + wide(side_in[block, span(piece)])
+        return value
+
+    greet(chips, pair, mine, spot, side)
+    if pair == 2:
+        for far in range(chips - 1, -1, -1):
+            for piece in range(PIECES):
+                for way in (1, -1) if far else (1,):
+                    block = spot + way * far
+
+                    @pl.when((block >= 0) & (block < chips))
+                    def _():
+                        side_copy(block, piece).start()
+
+    for far in range(chips - 1, 0, -1):
+        for piece in range(PIECES):
+            for way in (1, -1):
+                block = spot + way * far
+
+                @pl.when((block >= 0) & (block < chips))
+                def _():
+                    value = chip_sum(block, piece)
+                    total[block, span(piece)] = value.astype(total.dtype)
+                    if far < chips - 1:
+
+                        @pl.when((spot > 0) if way > 0 else (spot < chips - 1))
+                        def _():
+                            direction = 0 if way > 0 else 1
+                            line_copy(block, piece, way).wait_recv()
+                            total[block, span(piece)] = (
+                                wide(total[block, span(piece)])
+                                + wide(line_in[direction, block, span(piece)])
+                            ).astype(total.dtype)
+
+                    line_copy(block, piece, way).start()
+
+    for piece in range(PIECES):
+        total[spot, span(piece)] = chip_sum(spot, piece).astype(total.dtype)
+        for way in (1, -1):
+
+            @pl.when((spot > 0) if way > 0 else (spot < chips - 1))
+            def _():
+                direction = 0 if way > 0 else 1
+                line_copy(spot, piece, way).wait_recv()
+                total[spot, span(piece)] = (
+                    wide(total[spot, span(piece)]) + wide(line_in[direction, spot, span(piece)])
+                ).astype(total.dtype)
+
+        sum_ref[span(piece)] = total[spot, span(piece)]
+    for far in range(chips - 1, -1, -1):
+        for piece in range(PIECES):
+            for way in (1, -1) if far else (1,):
+                block = spot + way * far
+
+                @pl.when((block >= 0) & (block < chips))
+                def _():
+                    if far:
+                        line_copy(block, piece, way).wait_send()
+                    if pair == 2:
+                        side_copy(block, piece).wait_send()
+
+
+def gather_sum(parts):
+    count, height, width = parts.shape
+    pair = 2 if count % 2 == 0 else 1
+    chips = count // pair
+    return pl.pallas_call(
+        gather_sum_kernel,
+        out_shape=jax.ShapeDtypeStruct((height, width), parts.dtype),
+        in_specs=[pl.BlockSpec(memory_space=pltpu.VMEM)],
+        out_specs=pl.BlockSpec(memory_space=pltpu.VMEM),
+        scratch_shapes=[
+            pltpu.VMEM((chips, height, width), parts.dtype),
+            pltpu.VMEM((chips, height, width), parts.dtype),
+            pltpu.VMEM((2, chips, height, width), parts.dtype),
+            pltpu.SemaphoreType.DMA((chips, PIECES)),
+            pltpu.SemaphoreType.DMA((chips, PIECES)),
+            pltpu.SemaphoreType.DMA((chips, PIECES)),
+            pltpu.SemaphoreType.DMA((2, chips, PIECES)),
+        ],
+        compiler_params=pltpu.CompilerParams(collective_id=1, has_side_effects=True),
+    )(parts.reshape(chips, pair, height, width))
 
 
 def shifted(value, axis, steps):
@@ -147,8 +415,7 @@
         whole_rows = lax.all_gather(moe_input, "tensor", axis=1, tiled=True)
         place = placed[step_index]
         share = slot_share[step_index]
-        all_rows = lax.all_gather(whole_rows, "expert", axis=0, tiled=True)
-        all_rows = all_rows.reshape(sources, piece_list, full_width)
+        all_rows = spread(whole_rows)
         hidden_list = []
         for e in range(expert_local):
             rows_in = jnp.einsum(
@@ -183,10 +450,7 @@
                     preferred_element_type=jnp.float32,
                 )
                 total = term if total is None else total + term
-            total = total.astype(jnp.bfloat16).reshape(sources * piece_list, chunk)
-            routed_list.append(
-                lax.psum_scatter(total, "expert", scatter_dimension=0, tiled=True)
-            )
+            routed_list.append(gather_sum(total.astype(jnp.bfloat16)))
         routed = jnp.concatenate(routed_list, axis=1)
         routed = lax.psum_scatter(routed, "tensor", scatter_dimension=1, tiled=True).astype(
             jnp.float32

time: 374 us -> 359 us (0.960)
  the two profiles are of different devices: /device:TPU:0 before, /device:TPU:10 now
where the time goes in v2:
time: 359 us; the launch traced here: 352 us
  Pallas kernels  164 us (46%)
  matrix products  123 us (34%)
  other arithmetic  29.6 us (8%)
  waiting for transfers between devices  14.3 us (4%)
  blocking collectives  14.2 us (4%)
  local copies, waits for them, and re-layouts  5.24 us (1%)
    pallas_call x2, Pallas kernels, gather_sum(): pl.pallas_call(gather_sum_kernel, out_shape=jax.ShapeDtypeStruct((height,...  87.5 us
    pallas_call x2, Pallas kernels, spread(): pl.pallas_call(spread_kernel, out_shape=jax.ShapeDtypeStruct((chips, pair...  76.5 us
    dot_general x4, matrix products, shards(): jnp.dot(hidden_list[e], specialist_contract_factor[0, e][:, c * chunk:(c...  34.2 us
    dot_general x4, matrix products, shards(): jnp.einsum('jsr,jsd->jrd', place[:, e], down.reshape(sources, CAP, chunk)...  26.8 us
    dot_general x4, matrix products, shards(): jnp.dot(rows_in, specialist_switch_factor[0, e], preferred_element_type=j...  18.6 us
    ppermute x1, waiting for transfers between devices, shifted(): lax.ppermute(value, axis, [(source, source + steps) for source in range(i...  14.3 us
    all_gather x1, blocking collectives, shards(): lax.all_gather(jnp.swapaxes(shares_dense, 1, 2), 'expert', axis=1, tiled=...  14.2 us
    sub x2, other arithmetic, attend(): expd = jnp.where(visible[:, None, :], jnp.exp(scores - row_max), 0.0)  13.5 us
  transfers between devices with their start and end apart: 1, of which 1 were waited for; matrix products, arithmetic and copies ran while one was open for 0% of the time, Pallas kernels for 0%

profile of v2, /device:TPU:10, one launch (start us, length us, event | category | flops | bytes accessed | tf_op | source)
XLA Modules:
  0.0 351.7 jit_solution(3762905525939593566)
XLA Ops:
  2.6 14.2 %all-gather = f32[2,128,128]{2,1,0:T(8,128)S(1)} all-gather(f32[2,16,128]{2,1,0:T(8,128)S(1)} %bitcast.291), channel_id=2, replica_groups=mesh['groups'=2,'expert'=8,'section'=2,'tensor'=1] {'expert'}, dimensions={1}, use_global_device_ids=true | all-gather | bytes 147456 | tf_op jit(solution)/shard_map/all_gather | solution.py:352
  19.1 4.0 %fusion.130 = bf16[16,8,8,128]{3,2,1,0:T(8,128)(2,1)} fusion(bf16[1,2048,1024]{2,1,0:T(8,128)(2,1)} %param.24, bf16[1,128,2048]{2,1,0:T(8,128)(2,1)} %param.17, f32[2048]{0:T(1024)} %bitcast.292, f32[128]{0:T(128)S(1)} %add_rsqrt_fusion.5), kind=kOutput, calls=%fused_computation.110 | convolution fusion | flops 538050560 | bytes 4989440 | tf_op jit(solution)/shard_map/dot_general | solution.py:388
  30.6 4.6 %fusion.113 = f32[128,8,896]{2,0,1:T(8,128)} fusion(bf16[1,8,128,512]{3,2,1,0:T(8,128)(2,1)S(1)} %copy-done.7, bf16[128,512]{1,0:T(8,128)(2,1)S(1)} %multiply_convert_fusion.3, bf16[768,512]{1,0:T(8,128)(2,1)} %get-tuple-element.8, bf16[16,8,8,128]{3,2,1,0:T(8,128)(2,1)} %fusion.130), kind=kOutput, calls=%fused_computation.97 | convolution fusion | flops 1076101120 | bytes 5898240 | tf_op jit(solution)/shard_map/thl,kl->thk/dot_general | solution.py:298
  35.2 6.8 %fusion.209 = (f32[128,8]{0,1:T(8,128)S(1)}, f32[128,8,896]{2,0,1:T(8,128)}) fusion(f32[128,8,896]{2,0,1:T(8,128)} %fusion.113, pred[128,896]{1,0:T(8,128)(4,1)} %get-tuple-element.18), kind=kOutput, calls=%fused_computation.206 | output fusion | flops 6423423 | bytes 7458816 | tf_op jit(solution)/shard_map/sub | solution.py:305
  41.9 4.7 %fusion.126 = bf16[8,128,128]{1,2,0:T(8,128)(2,1)} fusion(f32[128,8,896]{2,0,1:T(8,128)} %get-tuple-element.24, f32[128,8]{0,1:T(8,128)S(1)} %get-tuple-element.23, bf16[1,8,512,128]{3,2,1,0:T(8,128)(2,1)} %param.26, bf16[128,512]{1,0:T(8,128)(2,1)S(1)} %multiply_convert_fusion.3, bf16[768,512]{1,0:T(8,128)(2,1)S(1)} %copy-done.10), kind=kOutput, calls=%fused_computation.108 | convolution fusion | flops 1078067200 | bytes 5902336 | tf_op jit(solution)/shard_map/thl,hld->thd/dot_general | solution.py:401
  50.8 38.0 %shard_map.163 = bf16[4,2,128,2048]{3,2,1,0:T(8,128)(2,1)} custom-call(bf16[128,2048]{1,0:T(8,128)(2,1)} %multiply_convert_fusion.1.own_ref), custom_call_target="tpu_custom_call" | custom-call | tf_op jit(solution)/shard_map/pallas_call | solution.py:143
  88.8 4.4 %convolution_convert_fusion.5 = bf16[8,64,2048]{2,1,0:T(8,128)(2,1)} fusion(bf16[8,128,2048]{2,1,0:T(8,128)(2,1)} %bitcast.272, pred[8,2,64,128]{3,2,0,1:T(32,128)(4,1)S(1)} %get-tuple-element.10), kind=kOutput, calls=%fused_computation.23 | convolution fusion | flops 269484032 | bytes 6356992 | tf_op jit(solution)/shard_map/jsr,jrd->jsd/dot_general | solution.py:421
  96.0 5.4 %fusion.18 = f32[512,704]{0,1:T(8,128)} fusion(bf16[512,2048]{1,0:T(8,128)(2,1)} %bitcast.276, bf16[1,2,2048,704]{2,3,1,0:T(8,128)(2,1)} %param.31), kind=kOutput, calls=%fused_computation.34 | convolution fusion | flops 1476395008 | bytes 6422528 | tf_op jit(solution)/shard_map/dot_general | solution.py:425
  101.4 4.7 %fusion.28 = f32[512,704]{0,1:T(8,128)} fusion(bf16[512,2048]{1,0:T(8,128)(2,1)S(1)} %bitcast.279, bf16[1,2,2048,704]{2,3,1,0:T(8,128)(2,1)} %param.31), kind=kOutput, calls=%fused_computation.44 | convolution fusion | flops 1476395008 | bytes 6422528 | tf_op jit(solution)/shard_map/dot_general | solution.py:425
  106.1 8.6 %convolution_convert_fusion.6 = bf16[512,2048]{1,0:T(8,128)(2,1)} fusion(bf16[1,2,704,2048]{3,2,1,0:T(8,128)(2,1)} %param.33, bf16[512,2048]{1,0:T(8,128)(2,1)} %bitcast.278, bf16[1,2,2048,704]{2,3,1,0:T(8,128)(2,1)} %param.32, f32[512,704]{0,1:T(8,128)} %fusion.28, f32[512]{0:T(512)S(1)} %mul.216), kind=kOutput, calls=%fused_computation.24 | convolution fusion | flops 2956361728 | bytes 11405312 | tf_op jit(solution)/shard_map/dot_general | solution.py:441
  114.6 6.1 %fusion.185 = f32[8,128,2048]{2,1,0:T(8,128)} fusion(bf16[8,64,2048]{2,1,0:T(8,128)(2,1)} %bitcast.286, pred[8,2,64,128]{3,2,0,1:T(32,128)(4,1)S(1)} %get-tuple-element.10), kind=kOutput, calls=%fused_computation.167 | convolution fusion | flops 268435456 | bytes 10551296 | tf_op jit(solution)/shard_map/jsr,jsd->jrd/dot_general | solution.py:446
  120.8 8.8 %convolution_convert_fusion.4 = bf16[512,2048]{1,0:T(8,128)(2,1)} fusion(bf16[1,2,704,2048]{3,2,1,0:T(8,128)(2,1)} %param.33, bf16[512,2048]{1,0:T(8,128)(2,1)} %bitcast.277, bf16[1,2,2048,704]{2,3,1,0:T(8,128)(2,1)} %param.32, f32[512,704]{0,1:T(8,128)} %fusion.18, f32[512]{0:T(512)S(1)} %mul.221), kind=kOutput, calls=%fused_computation.22 | convolution fusion | flops 2956361728 | bytes 11405312 | tf_op jit(solution)/shard_map/dot_general | solution.py:441
  129.6 7.3 %add_convert_fusion.1 = bf16[8,128,2048]{2,1,0:T(8,128)(2,1)} fusion(f32[8,128,2048]{2,1,0:T(8,128)} %fusion.185, bf16[8,64,2048]{2,1,0:T(8,128)(2,1)} %bitcast.282, pred[8,2,64,128]{3,2,0,1:T(32,128)(4,1)S(1)} %get-tuple-element.10), kind=kOutput, calls=%fused_computation.3 | convolution fusion | flops 272629760 | bytes 14745600 | tf_op jit(solution)/shard_map/jsr,jsd->jrd/dot_general | solution.py:446
  136.9 43.7 %shard_map.164 = bf16[128,2048]{1,0:T(8,128)(2,1)} custom-call(bf16[4,2,128,2048]{3,2,1,0:T(8,128)(2,1)} %bitcast.274), custom_call_target="tpu_custom_call" | custom-call | tf_op jit(solution)/shard_map/pallas_call | solution.py:263
  184.0 14.3 %collective-permute-done = bf16[128,2048]{1,0:T(8,128)(2,1)S(1)} collective-permute-done((bf16[128,2048]{1,0:T(8,128)(2,1)}, bf16[128,2048]{1,0:T(8,128)(2,1)S(1)}, u32[]{:S(2)}, u32[]{:S(2)}) %collective-permute-start) | collective-permute-done | bytes 524320 | tf_op jit(solution)/shard_map/ppermute | solution.py:284
  204.0 4.5 %fusion.115 = f32[128,8,896]{2,0,1:T(8,128)} fusion(bf16[1,8,128,512]{3,2,1,0:T(8,128)(2,1)S(1)} %copy-done.8, bf16[128,512]{1,0:T(8,128)(2,1)S(1)} %multiply_convert_fusion.2, bf16[768,512]{1,0:T(8,128)(2,1)} %get-tuple-element.7, bf16[16,8,8,128]{3,2,1,0:T(8,128)(2,1)S(1)} %fusion.127), kind=kOutput, calls=%fused_computation.99 | convolution fusion | flops 1076101120 | bytes 5898240 | tf_op jit(solution)/shard_map/thl,kl->thk/dot_general | solution.py:298
  208.5 6.8 %fusion.210 = (f32[128,8]{0,1:T(8,128)S(1)}, f32[128,8,896]{2,0,1:T(8,128)}) fusion(f32[128,8,896]{2,0,1:T(8,128)} %fusion.115, pred[128,896]{1,0:T(8,128)(4,1)S(1)} %copy-done.14), kind=kOutput, calls=%fused_computation.207 | output fusion | flops 6423423 | bytes 7458816 | tf_op jit(solution)/shard_map/sub | solution.py:305
  223.0 38.5 %shard_map.165 = bf16[4,2,128,2048]{3,2,1,0:T(8,128)(2,1)} custom-call(bf16[128,2048]{1,0:T(8,128)(2,1)} %multiply_convert_fusion.own_ref), custom_call_target="tpu_custom_call" | custom-call | tf_op jit(solution)/shard_map/pallas_call | solution.py:143
  265.7 5.7 %fusion.16 = f32[512,704]{0,1:T(8,128)} fusion(bf16[512,2048]{1,0:T(8,128)(2,1)S(1)} %bitcast.280, bf16[1,2,2048,704]{2,3,1,0:T(8,128)(2,1)} %param.31), kind=kOutput, calls=%fused_computation.32 | convolution fusion | flops 1476395008 | bytes 6422528 | tf_op jit(solution)/shard_map/dot_general | solution.py:425
  274.2 8.6 %convolution_convert_fusion.2 = bf16[512,2048]{1,0:T(8,128)(2,1)} fusion(bf16[1,2,704,2048]{3,2,1,0:T(8,128)(2,1)} %param.33, bf16[512,2048]{1,0:T(8,128)(2,1)} %bitcast.285, bf16[1,2,2048,704]{2,3,1,0:T(8,128)(2,1)} %param.32, f32[512,704]{0,1:T(8,128)} %fusion.26, f32[512]{0:T(512)S(1)} %mul.240), kind=kOutput, calls=%fused_computation.20 | convolution fusion | flops 2956361728 | bytes 11405312 | tf_op jit(solution)/shard_map/dot_general | solution.py:441
  282.8 6.1 %fusion.186 = f32[8,128,2048]{2,1,0:T(8,128)} fusion(bf16[8,64,2048]{2,1,0:T(8,128)(2,1)} %bitcast.287, pred[8,2,64,128]{3,2,0,1:T(32,128)(4,1)S(1)} %get-tuple-element.9), kind=kOutput, calls=%fused_computation.168 | convolution fusion | flops 268435456 | bytes 10551296 | tf_op jit(solution)/shard_map/jsr,jsd->jrd/dot_general | solution.py:446
  289.0 8.2 %convolution_convert_fusion = bf16[512,2048]{1,0:T(8,128)(2,1)} fusion(bf16[1,2,704,2048]{3,2,1,0:T(8,128)(2,1)} %param.33, bf16[512,2048]{1,0:T(8,128)(2,1)S(1)} %bitcast.281, bf16[1,2,2048,704]{2,3,1,0:T(8,128)(2,1)} %param.32, f32[512,704]{0,1:T(8,128)} %fusion.16, f32[512]{0:T(512)S(1)} %mul.245), kind=kOutput, calls=%fused_computation.18 | convolution fusion | flops 2956361728 | bytes 11405312 | tf_op jit(solution)/shard_map/dot_general | solution.py:441
  297.1 7.3 %add_convert_fusion = bf16[8,128,2048]{2,1,0:T(8,128)(2,1)} fusion(f32[8,128,2048]{2,1,0:T(8,128)} %fusion.186, bf16[8,64,2048]{2,1,0:T(8,128)(2,1)} %bitcast.283, pred[8,2,64,128]{3,2,0,1:T(32,128)(4,1)S(1)} %get-tuple-element.9), kind=kOutput, calls=%fused_computation.2 | convolution fusion | flops 272629760 | bytes 14745600 | tf_op jit(solution)/shard_map/jsr,jsd->jrd/dot_general | solution.py:446
  304.4 43.9 %shard_map.166 = bf16[128,2048]{1,0:T(8,128)(2,1)} custom-call(bf16[4,2,128,2048]{3,2,1,0:T(8,128)(2,1)} %bitcast.275), custom_call_target="tpu_custom_call" | custom-call | tf_op jit(solution)/shard_map/pallas_call | solution.py:263
  (110 shorter events, 46.2 us)
Async XLA Ops:
  0.0 23.1 %copy-start = (bf16[1,2048,512]{2,1,0:T(8,128)(2,1)S(1)}, bf16[1,2048,512]{2,1,0:T(8,128)(2,1)}, u32[]{:S(2)}) copy-start(bf16[1,2048,512]{2,1,0:T(8,128)(2,1)} %param.28) | copy-start | bytes 6291460
  0.0 23.1 %copy-start.23 = (s32[64]{0:T(128)}, s32[64]{0:T(128)S(1)}, u32[]{:S(2)}) copy-start(s32[64]{0:T(128)S(1)} %iota_add_fusion.1) | copy-start | bytes 772
  18.8 4.3 %copy-start.4 = (bf16[1,128,2048]{2,1,0:T(8,128)(2,1)S(1)}, bf16[1,128,2048]{2,1,0:T(8,128)(2,1)}, u32[]{:S(2)}) copy-start(bf16[1,128,2048]{2,1,0:T(8,128)(2,1)} %param.17) | copy-start | bytes 1572868
  18.8 4.3 %copy-start.18 = (f32[1,2048]{1,0:T(1,128)S(1)}, f32[1,2048]{1,0:T(1,128)}, u32[]{:S(2)}) copy-start(f32[1,2048]{1,0:T(1,128)} %param.23) | copy-start | bytes 24580
  19.1 5.8 %copy-start.13 = (bf16[2,1,1,768,512]{4,3,2,1,0:T(8,128)(2,1)S(1)}, bf16[2,1,1,768,512]{4,3,2,1,0:T(8,128)(2,1)}, u32[]{:S(2)}) copy-start(bf16[2,1,1,768,512]{4,3,2,1,0:T(8,128)(2,1)} %param.19) | copy-start | bytes 4718596
  23.1 7.4 %copy-start.7 = (bf16[1,8,128,512]{3,2,1,0:T(8,128)(2,1)S(1)}, bf16[1,8,128,512]{3,2,1,0:T(8,128)(2,1)}, u32[]{:S(2)}) copy-start(bf16[1,8,128,512]{3,2,1,0:T(8,128)(2,1)} %param.25) | copy-start | bytes 3145732
  35.2 6.8 %copy-start.10 = (bf16[768,512]{1,0:T(8,128)(2,1)S(1)}, bf16[768,512]{1,0:T(8,128)(2,1)}, u32[]{:S(2)}) copy-start(bf16[768,512]{1,0:T(8,128)(2,1)} %get-tuple-element.8) | copy-start | bytes 2359300
  46.6 3.2 copy-start.20
  88.8 4.4 %copy-start.3 = (bf16[4,2,128,2048]{3,2,1,0:T(8,128)(2,1)S(1)}, bf16[4,2,128,2048]{3,2,1,0:T(8,128)(2,1)}, u32[]{:S(2)}) copy-start(bf16[4,2,128,2048]{3,2,1,0:T(8,128)(2,1)} %shard_map.163) | copy-start | bytes 12582916
  96.0 5.4 %copy-start.11 = (bf16[8,64,2048]{2,1,0:T(8,128)(2,1)S(1)}, bf16[8,64,2048]{2,1,0:T(8,128)(2,1)}, u32[]{:S(2)}) copy-start(bf16[8,64,2048]{2,1,0:T(8,128)(2,1)} %convolution_convert_fusion.7) | copy-start | bytes 6291460
  180.5 19.0 %copy-start.19 = (f32[1,2048]{1,0:T(1,128)S(1)}, f32[1,2048]{1,0:T(1,128)}, u32[]{:S(2)}) copy-start(f32[1,2048]{1,0:T(1,128)} %param.23) | copy-start | bytes 24580
  182.5 15.7 %collective-permute-start = (bf16[128,2048]{1,0:T(8,128)(2,1)}, bf16[128,2048]{1,0:T(8,128)(2,1)S(1)}, u32[]{:S(2)}, u32[]{:S(2)}) collective-permute-start(bf16[128,2048]{1,0:T(8,128)(2,1)} %add_convert_fusion.3), channel_id=1, source_target_pairs={{0,1},{2,3},{4,5},{6,7},{8,9},{10,11},{12,13},{14,15},{16,17},{18,... | collective-permute-start | bytes 1572872 | tf_op jit(solution)/shard_map/ppermute | solution.py:284
  199.5 3.8 %copy-start.5 = (bf16[128,2048]{1,0:T(8,128)(2,1)}, bf16[128,2048]{1,0:T(8,128)(2,1)S(1)}, u32[]{:S(2)}) copy-start(bf16[128,2048]{1,0:T(8,128)(2,1)S(1)} %get-tuple-element.6) | copy-start | bytes 1572868
  199.6 3.8 %copy-start.22 = (f32[1,512]{1,0:T(1,128)S(1)}, f32[1,512]{1,0:T(1,128)}, u32[]{:S(2)}) copy-start(f32[1,512]{1,0:T(1,128)} %param.29) | copy-start | bytes 6148
  204.0 4.5 %copy-start.14 = (pred[128,896]{1,0:T(8,128)(4,1)S(1)}, pred[128,896]{1,0:T(8,128)(4,1)}, u32[]{:S(2)}) copy-start(pred[128,896]{1,0:T(8,128)(4,1)} %get-tuple-element.17) | copy-start | bytes 344068
  208.5 6.8 %copy-start.9 = (bf16[768,512]{1,0:T(8,128)(2,1)S(1)}, bf16[768,512]{1,0:T(8,128)(2,1)}, u32[]{:S(2)}) copy-start(bf16[768,512]{1,0:T(8,128)(2,1)} %get-tuple-element.7) | copy-start | bytes 2359300
  208.5 6.8 %copy-start.26 = (bf16[1,8,512,128]{3,2,1,0:T(8,128)(2,1)S(1)}, bf16[1,8,512,128]{3,2,1,0:T(8,128)(2,1)}, u32[]{:S(2)}) copy-start(bf16[1,8,512,128]{3,2,1,0:T(8,128)(2,1)} %param.26) | copy-start | bytes 3145732
  215.3 3.7 %copy-start.6 = (bf16[128,2048]{1,0:T(8,128)(2,1)S(1)}, bf16[128,2048]{1,0:T(8,128)(2,1)}, u32[]{:S(2)}) copy-start(bf16[128,2048]{1,0:T(8,128)(2,1)} %copy-done.5) | copy-start | bytes 1572868
  219.0 3.0 copy-start.21
  261.5 3.5 copy-start.2
  264.9 6.5 %slice-start = ((s8[5767168]{0:T(1024)(128)(4,1)}), s8[4194304]{0:T(1024)(128)(4,1)S(1)}, s32[]{:S(2)}) async-start(s8[5767168]{0:T(1024)(128)(4,1)} %bitcast.302), calls=%async_computation | async-start | bytes 8388608
  265.6 5.8 %copy-start.12 = (bf16[8,64,2048]{2,1,0:T(8,128)(2,1)}, bf16[8,64,2048]{2,1,0:T(8,128)(2,1)S(1)}, u32[]{:S(2)}) copy-start(bf16[8,64,2048]{2,1,0:T(8,128)(2,1)S(1)} %convolution_convert_fusion.3) | copy-start | bytes 6291460
  265.7 5.8 %slice-start.1 = ((s8[5767168]{0:T(1024)(128)(4,1)}), s8[1572864]{0:T(1024)(128)(4,1)S(1)}, s32[]{:S(2)}) async-start(s8[5767168]{0:T(1024)(128)(4,1)} %bitcast.302), calls=%async_computation.1 | async-start | bytes 3145728
  304.4 47.1 %copy-start.1 = (bf16[1,2048,512]{2,1,0:T(8,128)(2,1)S(1)}, bf16[1,2048,512]{2,1,0:T(8,128)(2,1)}, u32[]{:S(2)}) copy-start(bf16[1,2048,512]{2,1,0:T(8,128)(2,1)} %param.28) | copy-start | bytes 6291460
  (6 other events, 12.7 us)

commit v3 on v2

--- a/solution.py
+++ b/solution.py
@@ -6,7 +6,7 @@
 from jax.sharding import PartitionSpec as P
 
 CAP = 64
-RETURN_CHUNKS = 1
+RETURN_CHUNKS = 2
 
 
 epsilon = 1e-06
@@ -61,16 +61,25 @@
     )
 
 
-def spread_kernel(own_ref, all_ref, own_sem, line_send, line_recv, side_send, side_recv):
+def spread_kernel(
+    own_ref, small_ref, all_ref, small_all_ref, own_sem, line_send, line_recv, side_send, side_recv
+):
     chips, pair, mine, spot, side = place_on_line()
     step = own_ref.shape[0] // PIECES
     sibling = mine + 1 - 2 * side
 
     def rows(block, core, piece):
+        if piece == PIECES:
+            return small_all_ref.at[block, core]
         return all_ref.at[block, core, pl.ds(piece * step, step)]
 
+    def origin(block, piece):
+        if block is not None:
+            return rows(block, side, piece)
+        return small_ref if piece == PIECES else own_ref.at[pl.ds(piece * step, step)]
+
     def line_copy(block, piece, way):
-        source = own_ref.at[pl.ds(piece * step, step)] if block is None else rows(block, side, piece)
+        source = origin(block, piece)
         where = spot if block is None else block
         direction = 0 if way > 0 else 1
         return remote(
@@ -82,7 +91,7 @@
         )
 
     def side_copy(block, piece):
-        source = own_ref.at[pl.ds(piece * step, step)] if block is None else rows(block, side, piece)
+        source = origin(block, piece)
         where = spot if block is None else block
         return remote(
             source,
@@ -98,16 +107,18 @@
             act(line_copy(block, piece, way))
 
     greet(chips, pair, mine, spot, side)
-    for piece in range(PIECES):
+    for piece in range(PIECES + 1):
         for way in (1, -1):
             onward(None, piece, way, lambda copy: copy.start())
-    for piece in range(PIECES):
+    for piece in range(PIECES + 1):
         if pair == 2:
             side_copy(None, piece).start()
-    keep = pltpu.make_async_copy(own_ref, all_ref.at[spot, side], own_sem)
+    keep = pltpu.make_async_copy(own_ref, all_ref.at[spot, side], own_sem.at[0])
     keep.start()
+    keep_small = pltpu.make_async_copy(small_ref, small_all_ref.at[spot, side], own_sem.at[1])
+    keep_small.start()
     for far in range(1, chips):
-        for piece in range(PIECES):
+        for piece in range(PIECES + 1):
             for way in (1, -1):
                 block = spot - way * far
 
@@ -119,13 +130,14 @@
                         side_copy(block, piece).start()
 
     keep.wait()
-    for piece in range(PIECES):
+    keep_small.wait()
+    for piece in range(PIECES + 1):
         for way in (1, -1):
             onward(None, piece, way, lambda copy: copy.wait_send())
         if pair == 2:
             side_copy(None, piece).wait()
     for far in range(1, chips):
-        for piece in range(PIECES):
+        for piece in range(PIECES + 1):
             for way in (1, -1):
                 block = spot - way * far
 
@@ -136,42 +148,41 @@
                         side_copy(block, piece).wait()
 
 
-def spread(own):
+def spread(own, small):
     count = lax.axis_size("expert")
     pair = 2 if count % 2 == 0 else 1
     chips = count // pair
-    result = pl.pallas_call(
+    result, small_result = pl.pallas_call(
         spread_kernel,
-        out_shape=jax.ShapeDtypeStruct((chips, pair) + own.shape, own.dtype),
-        in_specs=[pl.BlockSpec(memory_space=pltpu.VMEM)],
-        out_specs=pl.BlockSpec(memory_space=pltpu.VMEM),
+        out_shape=[
+            jax.ShapeDtypeStruct((chips, pair) + own.shape, own.dtype),
+            jax.ShapeDtypeStruct((chips, pair) + small.shape, small.dtype),
+        ],
+        in_specs=[pl.BlockSpec(memory_space=pltpu.VMEM)] * 2,
+        out_specs=[pl.BlockSpec(memory_space=pltpu.VMEM)] * 2,
         scratch_shapes=[
-            pltpu.SemaphoreType.DMA,
-            pltpu.SemaphoreType.DMA((2, chips, PIECES)),
-            pltpu.SemaphoreType.DMA((chips, PIECES)),
-            pltpu.SemaphoreType.DMA((chips, PIECES)),
-            pltpu.SemaphoreType.DMA((chips, PIECES)),
+            pltpu.SemaphoreType.DMA((2,)),
+            pltpu.SemaphoreType.DMA((2, chips, PIECES + 1)),
+            pltpu.SemaphoreType.DMA((chips, PIECES + 1)),
+            pltpu.SemaphoreType.DMA((chips, PIECES + 1)),
+            pltpu.SemaphoreType.DMA((chips, PIECES + 1)),
         ],
         compiler_params=pltpu.CompilerParams(collective_id=0, has_side_effects=True),
-    )(own)
-    return result.reshape((count,) + own.shape)
-
-
-def gather_sum_kernel(
-    part_ref, sum_ref, side_in, total, line_in, side_send, side_recv, line_send, line_recv
-):
+    )(own, small)
+    return result.reshape((count,) + own.shape), small_result.reshape((count,) + small.shape)
+
+
+def gather_sum_kernel(*refs):
+    part_refs, refs = refs[:RETURN_CHUNKS], refs[RETURN_CHUNKS:]
+    sum_ref, side_in, total, line_in, side_send, side_recv, line_send, line_recv = refs
     chips, pair, mine, spot, side = place_on_line()
-    height = part_ref.shape[2]
-    step = height // PIECES
+    chunk = part_refs[0].shape[3]
     sibling = mine + 1 - 2 * side
-
-    def span(piece):
-        return pl.ds(piece * step, step)
 
     def side_copy(block, piece):
         return remote(
-            part_ref.at[block, 1 - side, span(piece)],
-            side_in.at[block, span(piece)],
+            part_refs[piece].at[block, 1 - side],
+            side_in.at[block, piece],
             side_send.at[block, piece],
             side_recv.at[block, piece],
             sibling,
@@ -180,8 +191,8 @@
     def line_copy(block, piece, way):
         direction = 0 if way > 0 else 1
         return remote(
-            total.at[block, span(piece)],
-            line_in.at[direction, block, span(piece)],
+            total.at[block, piece],
+            line_in.at[direction, block, piece],
             line_send.at[block, piece],
             line_recv.at[direction, block, piece],
             mine + way * pair,
@@ -191,16 +202,16 @@
         return value.astype(jnp.float32)
 
     def chip_sum(block, piece):
-        value = wide(part_ref[block, side, span(piece)])
+        value = wide(part_refs[piece][block, side])
         if pair == 2:
             side_copy(block, piece).wait_recv()
-            value = value + wide(side_in[block, span(piece)])
+            value = value + wide(side_in[block, piece])
         return value
 
     greet(chips, pair, mine, spot, side)
     if pair == 2:
         for far in range(chips - 1, -1, -1):
-            for piece in range(PIECES):
+            for piece in range(RETURN_CHUNKS):
                 for way in (1, -1) if far else (1,):
                     block = spot + way * far
 
@@ -209,42 +220,42 @@
                         side_copy(block, piece).start()
 
     for far in range(chips - 1, 0, -1):
-        for piece in range(PIECES):
+        for piece in range(RETURN_CHUNKS):
             for way in (1, -1):
                 block = spot + way * far
 
                 @pl.when((block >= 0) & (block < chips))
                 def _():
                     value = chip_sum(block, piece)
-                    total[block, span(piece)] = value.astype(total.dtype)
+                    total[block, piece] = value.astype(total.dtype)
                     if far < chips - 1:
 
                         @pl.when((spot > 0) if way > 0 else (spot < chips - 1))
                         def _():
                             direction = 0 if way > 0 else 1
                             line_copy(block, piece, way).wait_recv()
-                            total[block, span(piece)] = (
-                                wide(total[block, span(piece)])
-                                + wide(line_in[direction, block, span(piece)])
+                            total[block, piece] = (
+                                wide(total[block, piece])
+                                + wide(line_in[direction, block, piece])
                             ).astype(total.dtype)
 
                     line_copy(block, piece, way).start()
 
-    for piece in range(PIECES):
-        total[spot, span(piece)] = chip_sum(spot, piece).astype(total.dtype)
+    for piece in range(RETURN_CHUNKS):
+        total[spot, piece] = chip_sum(spot, piece).astype(total.dtype)
         for way in (1, -1):
 
             @pl.when((spot > 0) if way > 0 else (spot < chips - 1))
             def _():
                 direction = 0 if way > 0 else 1
                 line_copy(spot, piece, way).wait_recv()
-                total[spot, span(piece)] = (
-                    wide(total[spot, span(piece)]) + wide(line_in[direction, spot, span(piece)])
+                total[spot, piece] = (
+                    wide(total[spot, piece]) + wide(line_in[direction, spot, piece])
                 ).astype(total.dtype)
 
-        sum_ref[span(piece)] = total[spot, span(piece)]
+        sum_ref[:, pl.ds(piece * chunk, chunk)] = total[spot, piece]
     for far in range(chips - 1, -1, -1):
-        for piece in range(PIECES):
+        for piece in range(RETURN_CHUNKS):
             for way in (1, -1) if far else (1,):
                 block = spot + way * far
 
@@ -257,25 +268,27 @@
 
 
 def gather_sum(parts):
-    count, height, width = parts.shape
+    count, height, chunk = parts[0].shape
+    pieces = len(parts)
+    kind = parts[0].dtype
     pair = 2 if count % 2 == 0 else 1
     chips = count // pair
     return pl.pallas_call(
         gather_sum_kernel,
-        out_shape=jax.ShapeDtypeStruct((height, width), parts.dtype),
-        in_specs=[pl.BlockSpec(memory_space=pltpu.VMEM)],
+        out_shape=jax.ShapeDtypeStruct((height, pieces * chunk), kind),
+        in_specs=[pl.BlockSpec(memory_space=pltpu.VMEM)] * pieces,
         out_specs=pl.BlockSpec(memory_space=pltpu.VMEM),
         scratch_shapes=[
-            pltpu.VMEM((chips, height, width), parts.dtype),
-            pltpu.VMEM((chips, height, width), parts.dtype),
-            pltpu.VMEM((2, chips, height, width), parts.dtype),
-            pltpu.SemaphoreType.DMA((chips, PIECES)),
-            pltpu.SemaphoreType.DMA((chips, PIECES)),
-            pltpu.SemaphoreType.DMA((chips, PIECES)),
-            pltpu.SemaphoreType.DMA((2, chips, PIECES)),
+            pltpu.VMEM((chips, pieces, height, chunk), kind),
+            pltpu.VMEM((chips, pieces, height, chunk), kind),
+            pltpu.VMEM((2, chips, pieces, height, chunk), kind),
+            pltpu.SemaphoreType.DMA((chips, pieces)),
+            pltpu.SemaphoreType.DMA((chips, pieces)),
+            pltpu.SemaphoreType.DMA((chips, pieces)),
+            pltpu.SemaphoreType.DMA((2, chips, pieces)),
         ],
         compiler_params=pltpu.CompilerParams(collective_id=1, has_side_effects=True),
-    )(parts.reshape(chips, pair, height, width))
+    )(*[part.reshape(chips, pair, height, chunk) for part in parts])
 
 
 def shifted(value, axis, steps):
@@ -349,27 +362,12 @@
         ),
         axis=2,
     )
-    shares_all = lax.all_gather(
-        jnp.swapaxes(shares_dense, 1, 2), "expert", axis=1, tiled=False
-    )
-    mine = lax.dynamic_slice_in_dim(
-        shares_all, lax.axis_index("expert") * expert_local, expert_local, axis=2
-    )
-    chosen = mine > 0.0
+    shares_dense = jnp.swapaxes(shares_dense, 1, 2)
     earlier_or_same = (
         lax.broadcasted_iota(jnp.int32, (piece_list, piece_list), 0)
         <= lax.broadcasted_iota(jnp.int32, (piece_list, piece_list), 1)
     ).astype(jnp.bfloat16)
-    rank = jnp.einsum(
-        "tjer,rq->tjeq",
-        chosen.astype(jnp.bfloat16),
-        earlier_or_same,
-        preferred_element_type=jnp.float32,
-    ).astype(jnp.int32)
-    slots = lax.broadcasted_iota(jnp.int32, (1, 1, 1, CAP, 1), 3) + 1
-    at_slot = (rank[..., None, :] == slots) & chosen[..., None, :]
-    placed = at_slot.astype(jnp.bfloat16)
-    slot_share = jnp.sum(jnp.where(at_slot, mine[..., None, :], 0.0), axis=-1)
+    slots = lax.broadcasted_iota(jnp.int32, (1, 1, CAP, 1), 2) + 1
     outputs = []
     present_carry = opening_residual[0]
     section_out = present_carry
@@ -413,9 +411,20 @@
             * specialist_scale_factor[0]
         ).astype(jnp.bfloat16)
         whole_rows = lax.all_gather(moe_input, "tensor", axis=1, tiled=True)
-        place = placed[step_index]
-        share = slot_share[step_index]
-        all_rows = spread(whole_rows)
+        all_rows, all_shares = spread(whole_rows, shares_dense[step_index])
+        mine = lax.dynamic_slice_in_dim(
+            all_shares, lax.axis_index("expert") * expert_local, expert_local, axis=1
+        )
+        chosen = mine > 0.0
+        rank = jnp.einsum(
+            "jer,rq->jeq",
+            chosen.astype(jnp.bfloat16),
+            earlier_or_same,
+            preferred_element_type=jnp.float32,
+        ).astype(jnp.int32)
+        at_slot = (rank[..., None, :] == slots) & chosen[..., None, :]
+        place = at_slot.astype(jnp.bfloat16)
+        share = jnp.sum(jnp.where(at_slot, mine[..., None, :], 0.0), axis=-1)
         hidden_list = []
         for e in range(expert_local):
             rows_in = jnp.einsum(
@@ -450,8 +459,8 @@
                     preferred_element_type=jnp.float32,
                 )
                 total = term if total is None else total + term
-            routed_list.append(gather_sum(total.astype(jnp.bfloat16)))
-        routed = jnp.concatenate(routed_list, axis=1)
+            routed_list.append(total.astype(jnp.bfloat16))
+        routed = gather_sum(routed_list)
         routed = lax.psum_scatter(routed, "tensor", scatter_dimension=1, tiled=True).astype(
             jnp.float32
         )

time: 359 us -> 330 us (0.919)
  matrix products: 123 us -> 99.6 us
  blocking collectives: 14.2 us -> 0 us
  local copies, waits for them, and re-layouts: 5.24 us -> 12.7 us
    dot_general x4 -> x8, matrix products: 34.2 us -> 11.1 us  [shards(): jnp.dot(hidden_list[e], specialist_contract_factor[0, e][:, c * chunk:(c...]
    dot_general x1 -> x6, matrix products: 0.14 us -> 15.5 us  [the longest x4 15.2 us: shards(): jnp.dot(rows_in, specialist_widen_factor[0, e], preferred_element_type=jn...]
    dot_general x4 -> x8, matrix products: 26.8 us -> 11.9 us  [shards(): jnp.einsum('jsr,jsd->jrd', place[:, e], down.reshape(sources, CAP, chunk)...]
    all_gather x1 -> x0, blocking collectives: 14.2 us -> none  [shards(): lax.all_gather(jnp.swapaxes(shares_dense, 1, 2), 'expert', axis=1, tiled=...]
    squeeze x2, local copies, waits for them, and re-layouts: 0.04 us -> 6.05 us  [the longest x1 5.44 us: shards(): specialist_contract_factor[0, e][:, c * chunk:(c + 1) * chunk]]
where the time goes in v3:
time: 330 us; the launch traced here: 324 us
  Pallas kernels  165 us (50%)
  matrix products  99.6 us (30%)
  other arithmetic  29.7 us (9%)
  waiting for transfers between devices  14.4 us (4%)
  local copies, waits for them, and re-layouts  12.7 us (4%)
    pallas_call x2, Pallas kernels, gather_sum(): pl.pallas_call(gather_sum_kernel, out_shape=jax.ShapeDtypeStruct((height,...  87.4 us
    pallas_call x2, Pallas kernels, spread(): pl.pallas_call(spread_kernel, out_shape=[jax.ShapeDtypeStruct((chips, pai...  78 us
    dot_general x4, matrix products, shards(): jnp.dot(rows_in, specialist_switch_factor[0, e], preferred_element_type=j...  17.4 us
    dot_general x4, matrix products, shards(): jnp.dot(rows_in, specialist_widen_factor[0, e], preferred_element_type=jn...  15.2 us
    ppermute x1, waiting for transfers between devices, shifted(): lax.ppermute(value, axis, [(source, source + steps) for source in range(i...  14.4 us
    sub x2, other arithmetic, attend(): expd = jnp.where(visible[:, None, :], jnp.exp(scores - row_max), 0.0)  13.5 us
    dot_general x4, matrix products, shards(): jnp.einsum('jsr,jrd->jsd', place[:, e], all_rows, preferred_element_type=...  12.8 us
    dot_general x8, matrix products, shards(): jnp.einsum('jsr,jsd->jrd', place[:, e], down.reshape(sources, CAP, chunk)...  11.9 us
  transfers between devices with their start and end apart: 1, of which 1 were waited for; matrix products, arithmetic and copies ran while one was open for 0% of the time, Pallas kernels for 0%

profile of v3, /device:TPU:10, one launch (start us, length us, event | category | flops | bytes accessed | tf_op | source)
XLA Modules:
  0.0 323.9 jit_solution(1863049322862959544)
XLA Ops:
  4.4 3.2 %fusion.130 = bf16[16,8,8,128]{3,2,1,0:T(8,128)(2,1)S(1)} fusion(bf16[1,2048,1024]{2,1,0:T(8,128)(2,1)} %param.24, bf16[1,128,2048]{2,1,0:T(8,128)(2,1)} %param.17, f32[2048]{0:T(1024)} %bitcast.302, f32[128]{0:T(128)S(1)} %add_rsqrt_fusion.5), kind=kOutput, calls=%fused_computation.118 | convolution fusion | flops 538050560 | bytes 4989440 | tf_op jit(solution)/shard_map/dot_general | solution.py:386
  15.1 4.5 %fusion.105 = f32[128,8,896]{2,0,1:T(8,128)} fusion(bf16[1,8,128,512]{3,2,1,0:T(8,128)(2,1)S(1)} %copy-done.7, bf16[128,512]{1,0:T(8,128)(2,1)S(1)} %multiply_convert_fusion.3, bf16[768,512]{1,0:T(8,128)(2,1)} %get-tuple-element.18, bf16[16,8,8,128]{3,2,1,0:T(8,128)(2,1)S(1)} %fusion.130), kind=kOutput, calls=%fused_computation.97 | convolution fusion | flops 1076101120 | bytes 5898240 | tf_op jit(solution)/shard_map/thl,kl->thk/dot_general | solution.py:311
  19.6 6.8 %fusion.192 = (f32[128,8]{0,1:T(8,128)S(1)}, f32[128,8,896]{2,0,1:T(8,128)}) fusion(f32[128,8,896]{2,0,1:T(8,128)} %fusion.105, pred[128,896]{1,0:T(8,128)(4,1)} %get-tuple-element.26), kind=kOutput, calls=%fused_computation.207 | output fusion | flops 6423423 | bytes 7458816 | tf_op jit(solution)/shard_map/sub | solution.py:318
  26.4 3.9 %fusion.126 = bf16[8,128,128]{1,2,0:T(8,128)(2,1)S(1)} fusion(f32[128,8,896]{2,0,1:T(8,128)} %get-tuple-element.32, f32[128,8]{0,1:T(8,128)S(1)} %get-tuple-element.31, bf16[1,8,512,128]{3,2,1,0:T(8,128)(2,1)} %param.26, bf16[128,512]{1,0:T(8,128)(2,1)S(1)} %multiply_convert_fusion.3, bf16[768,512]{1,0:T(8,128)(2,1)S(1)} %copy-done.10), kind=kOutput, calls=%fused_computation.116 | convolution fusion | flops 1078067200 | bytes 5902336 | tf_op jit(solution)/shard_map/thl,hld->thd/dot_general | solution.py:399
  34.5 39.3 %shard_map.163 = (bf16[4,2,128,2048]{3,2,1,0:T(8,128)(2,1)}, f32[4,2,16,128]{3,2,1,0:T(8,128)}) custom-call(bf16[128,2048]{1,0:T(8,128)(2,1)} %multiply_convert_fusion.1.own_ref, f32[16,128]{1,0:T(8,128)} %get-tuple-element.20.small_ref), custom_call_target="tpu_custom_call" | custom-call | tf_op jit(solution)/shard_map/pallas_call | solution.py:155
  74.9 4.4 %convolution_convert_fusion.2 = bf16[8,64,2048]{2,1,0:T(8,128)(2,1)} fusion(bf16[8,128,2048]{2,1,0:T(8,128)(2,1)} %bitcast.277, pred[8,2,64,128]{3,2,0,1:T(32,128)(4,1)S(1)} %compare_and_fusion.1), kind=kOutput, calls=%fused_computation.22 | convolution fusion | flops 269484032 | bytes 6356992 | tf_op jit(solution)/shard_map/jsr,jrd->jsd/dot_general | solution.py:430
  81.7 5.4 %slice_bitcast_fusion = (bf16[704,2048]{1,0:T(8,128)(2,1)S(1)}, bf16[704,2048]{1,0:T(8,128)(2,1)}) fusion(bf16[1,2,704,2048]{3,2,1,0:T(8,128)(2,1)} %param.33), kind=kLoop, calls=%fused_computation.40 | loop fusion | bytes 11534336 | tf_op jit(solution)/shard_map/squeeze | solution.py:452
  87.2 4.5 %fusion.16 = f32[512,704]{0,1:T(8,128)S(1)} fusion(bf16[512,2048]{1,0:T(8,128)(2,1)S(1)} %bitcast.287, bf16[1,2,2048,704]{2,3,1,0:T(8,128)(2,1)} %param.31), kind=kOutput, calls=%fused_computation.30 | convolution fusion | flops 1476395008 | bytes 6422528 | tf_op jit(solution)/shard_map/dot_general | solution.py:434
  91.7 3.7 %fusion.98 = bf16[512,704]{0,1:T(8,128)(2,1)S(1)} fusion(bf16[512,2048]{1,0:T(8,128)(2,1)S(1)} %bitcast.288, bf16[1,2,2048,704]{2,3,1,0:T(8,128)(2,1)} %param.32, f32[512,704]{0,1:T(8,128)S(1)} %fusion.16, f32[512]{0:T(512)S(1)} %mul.222), kind=kOutput, calls=%fused_computation.94 | convolution fusion | flops 1478918144 | bytes 7145472 | tf_op jit(solution)/shard_map/dot_general | solution.py:437
  99.5 4.3 %fusion.24 = f32[512,704]{0,1:T(8,128)S(1)} fusion(bf16[512,2048]{1,0:T(8,128)(2,1)} %bitcast.283, bf16[1,2,2048,704]{2,3,1,0:T(8,128)(2,1)} %param.31), kind=kOutput, calls=%fused_computation.38 | convolution fusion | flops 1476395008 | bytes 6422528 | tf_op jit(solution)/shard_map/dot_general | solution.py:434
  103.8 3.8 %fusion.92 = bf16[512,704]{0,1:T(8,128)(2,1)S(1)} fusion(bf16[512,2048]{1,0:T(8,128)(2,1)S(1)} %bitcast.284, bf16[1,2,2048,704]{2,3,1,0:T(8,128)(2,1)} %param.32, f32[512,704]{0,1:T(8,128)S(1)} %fusion.24, f32[512]{0:T(512)S(1)} %mul.217), kind=kOutput, calls=%fused_computation.92 | convolution fusion | flops 1478918144 | bytes 7145472 | tf_op jit(solution)/shard_map/dot_general | solution.py:437
  116.1 43.6 %shard_map.164 = bf16[128,2048]{1,0:T(8,128)(2,1)} custom-call(bf16[4,2,128,1024]{3,2,1,0:T(8,128)(2,1)} %bitcast.279, bf16[4,2,128,1024]{3,2,1,0:T(8,128)(2,1)} %bitcast.281), custom_call_target="tpu_custom_call" | custom-call | tf_op jit(solution)/shard_map/pallas_call | solution.py:276
  163.0 14.4 %collective-permute-done = bf16[128,2048]{1,0:T(8,128)(2,1)S(1)} collective-permute-done((bf16[128,2048]{1,0:T(8,128)(2,1)}, bf16[128,2048]{1,0:T(8,128)(2,1)S(1)}, u32[]{:S(2)}, u32[]{:S(2)}) %collective-permute-start) | collective-permute-done | bytes 524320 | tf_op jit(solution)/shard_map/ppermute | solution.py:297
  178.8 3.2 fusion.127
  183.2 4.5 %fusion.107 = f32[128,8,896]{2,0,1:T(8,128)} fusion(bf16[1,8,128,512]{3,2,1,0:T(8,128)(2,1)S(1)} %copy-done.8, bf16[128,512]{1,0:T(8,128)(2,1)S(1)} %multiply_convert_fusion.2, bf16[768,512]{1,0:T(8,128)(2,1)} %get-tuple-element.17, bf16[16,8,8,128]{3,2,1,0:T(8,128)(2,1)S(1)} %fusion.127), kind=kOutput, calls=%fused_computation.99 | convolution fusion | flops 1076101120 | bytes 5898240 | tf_op jit(solution)/shard_map/thl,kl->thk/dot_general | solution.py:311
  187.7 6.8 %fusion.193 = (f32[128,8]{0,1:T(8,128)S(1)}, f32[128,8,896]{2,0,1:T(8,128)}) fusion(f32[128,8,896]{2,0,1:T(8,128)} %fusion.107, pred[128,896]{1,0:T(8,128)(4,1)S(1)} %copy-done.23), kind=kOutput, calls=%fused_computation.208 | output fusion | flops 6423423 | bytes 7458816 | tf_op jit(solution)/shard_map/sub | solution.py:318
  194.5 3.7 %fusion.125 = bf16[8,128,128]{1,2,0:T(8,128)(2,1)S(1)} fusion(f32[128,8,896]{2,0,1:T(8,128)} %get-tuple-element.38, f32[128,8]{0,1:T(8,128)S(1)} %get-tuple-element.37, bf16[1,8,512,128]{3,2,1,0:T(8,128)(2,1)S(1)} %copy-done.29, bf16[128,512]{1,0:T(8,128)(2,1)S(1)} %multiply_convert_fusion.2, bf16[768,512]{1,0:T(8,128)(2,1)S(1)} %copy-done.9), kind=kOutput, calls=%fused_computation.115 | convolution fusion | flops 1078067200 | bytes 5902336 | tf_op jit(solution)/shard_map/thl,hld->thd/dot_general | solution.py:399
  202.2 38.7 %shard_map.165 = (bf16[4,2,128,2048]{3,2,1,0:T(8,128)(2,1)}, f32[4,2,16,128]{3,2,1,0:T(8,128)}) custom-call(bf16[128,2048]{1,0:T(8,128)(2,1)} %multiply_convert_fusion.own_ref, f32[16,128]{1,0:T(8,128)} %get-tuple-element.19.small_ref), custom_call_target="tpu_custom_call" | custom-call | tf_op jit(solution)/shard_map/pallas_call | solution.py:155
  242.0 4.4 %convolution_convert_fusion = bf16[8,64,2048]{2,1,0:T(8,128)(2,1)} fusion(bf16[8,128,2048]{2,1,0:T(8,128)(2,1)} %bitcast.275, pred[8,2,64,128]{3,2,0,1:T(32,128)(4,1)S(1)} %compare_and_fusion), kind=kOutput, calls=%fused_computation.20 | convolution fusion | flops 269484032 | bytes 6356992 | tf_op jit(solution)/shard_map/jsr,jrd->jsd/dot_general | solution.py:430
  248.8 4.3 %fusion.14 = f32[512,704]{0,1:T(8,128)S(1)} fusion(bf16[512,2048]{1,0:T(8,128)(2,1)} %bitcast.289, bf16[1,2,2048,704]{2,3,1,0:T(8,128)(2,1)} %param.31), kind=kOutput, calls=%fused_computation.28 | convolution fusion | flops 1476395008 | bytes 6422528 | tf_op jit(solution)/shard_map/dot_general | solution.py:434
  253.1 3.8 %fusion.101 = bf16[512,704]{0,1:T(8,128)(2,1)S(1)} fusion(bf16[512,2048]{1,0:T(8,128)(2,1)S(1)} %bitcast.290, bf16[1,2,2048,704]{2,3,1,0:T(8,128)(2,1)} %param.32, f32[512,704]{0,1:T(8,128)S(1)} %fusion.14, f32[512]{0:T(512)S(1)} %mul.246), kind=kOutput, calls=%fused_computation.95 | convolution fusion | flops 1478918144 | bytes 7145472 | tf_op jit(solution)/shard_map/dot_general | solution.py:437
  260.0 4.3 %fusion.22 = f32[512,704]{0,1:T(8,128)S(1)} fusion(bf16[512,2048]{1,0:T(8,128)(2,1)} %bitcast.285, bf16[1,2,2048,704]{2,3,1,0:T(8,128)(2,1)} %param.31), kind=kOutput, calls=%fused_computation.36 | convolution fusion | flops 1476395008 | bytes 6422528 | tf_op jit(solution)/shard_map/dot_general | solution.py:434
  264.3 3.9 %fusion.95 = bf16[512,704]{0,1:T(8,128)(2,1)S(1)} fusion(bf16[512,2048]{1,0:T(8,128)(2,1)S(1)} %bitcast.286, bf16[1,2,2048,704]{2,3,1,0:T(8,128)(2,1)} %param.32, f32[512,704]{0,1:T(8,128)S(1)} %fusion.22, f32[512]{0:T(512)S(1)} %mul.241), kind=kOutput, calls=%fused_computation.93 | convolution fusion | flops 1478918144 | bytes 7145472 | tf_op jit(solution)/shard_map/dot_general | solution.py:437
  276.7 43.8 %shard_map.166 = bf16[128,2048]{1,0:T(8,128)(2,1)} custom-call(bf16[4,2,128,1024]{3,2,1,0:T(8,128)(2,1)} %bitcast.282, bf16[4,2,128,1024]{3,2,1,0:T(8,128)(2,1)} %bitcast.280), custom_call_target="tpu_custom_call" | custom-call | tf_op jit(solution)/shard_map/pallas_call | solution.py:276
  (129 shorter events, 59.9 us)
Async XLA Ops:
  0.0 7.7 %copy-start = (bf16[1,2048,512]{2,1,0:T(8,128)(2,1)S(1)}, bf16[1,2048,512]{2,1,0:T(8,128)(2,1)}, u32[]{:S(2)}) copy-start(bf16[1,2048,512]{2,1,0:T(8,128)(2,1)} %param.28) | copy-start | bytes 6291460
  0.0 7.7 %copy-start.4 = (bf16[1,128,2048]{2,1,0:T(8,128)(2,1)S(1)}, bf16[1,128,2048]{2,1,0:T(8,128)(2,1)}, u32[]{:S(2)}) copy-start(bf16[1,128,2048]{2,1,0:T(8,128)(2,1)} %param.17) | copy-start | bytes 1572868
  0.0 7.7 %copy-start.24 = (f32[1,2048]{1,0:T(1,128)S(1)}, f32[1,2048]{1,0:T(1,128)}, u32[]{:S(2)}) copy-start(f32[1,2048]{1,0:T(1,128)} %param.23) | copy-start | bytes 24580
  4.4 5.0 %copy-start.19 = (bf16[2,1,1,768,512]{4,3,2,1,0:T(8,128)(2,1)S(1)}, bf16[2,1,1,768,512]{4,3,2,1,0:T(8,128)(2,1)}, u32[]{:S(2)}) copy-start(bf16[2,1,1,768,512]{4,3,2,1,0:T(8,128)(2,1)} %param.19) | copy-start | bytes 4718596
  7.7 4.9 %copy-start.26 = (f32[1,512]{1,0:T(1,128)S(1)}, f32[1,512]{1,0:T(1,128)}, u32[]{:S(2)}) copy-start(f32[1,512]{1,0:T(1,128)} %param.29) | copy-start | bytes 6148
  8.9 6.2 %copy-start.7 = (bf16[1,8,128,512]{3,2,1,0:T(8,128)(2,1)S(1)}, bf16[1,8,128,512]{3,2,1,0:T(8,128)(2,1)}, u32[]{:S(2)}) copy-start(bf16[1,8,128,512]{3,2,1,0:T(8,128)(2,1)} %param.25) | copy-start | bytes 3145732
  19.6 6.8 %copy-start.10 = (bf16[768,512]{1,0:T(8,128)(2,1)S(1)}, bf16[768,512]{1,0:T(8,128)(2,1)}, u32[]{:S(2)}) copy-start(bf16[768,512]{1,0:T(8,128)(2,1)} %get-tuple-element.18) | copy-start | bytes 2359300
  30.4 44.4 %copy-start.27 = (s32[64]{0:T(128)S(1)}, s32[64]{0:T(128)}, u32[]{:S(2)}) copy-start(s32[64]{0:T(128)} %iota_add_fusion.1) | copy-start | bytes 772
  74.9 4.4 %copy-start.3 = (bf16[4,2,128,2048]{3,2,1,0:T(8,128)(2,1)S(1)}, bf16[4,2,128,2048]{3,2,1,0:T(8,128)(2,1)}, u32[]{:S(2)}) copy-start(bf16[4,2,128,2048]{3,2,1,0:T(8,128)(2,1)} %get-tuple-element.10) | copy-start | bytes 12582916
  81.7 5.4 %copy-start.17 = (bf16[8,64,2048]{2,1,0:T(8,128)(2,1)S(1)}, bf16[8,64,2048]{2,1,0:T(8,128)(2,1)}, u32[]{:S(2)}) copy-start(bf16[8,64,2048]{2,1,0:T(8,128)(2,1)} %convolution_convert_fusion.2) | copy-start | bytes 6291460
  87.2 10.3 %copy-start.13 = (bf16[704,2048]{1,0:T(8,128)(2,1)}, bf16[704,2048]{1,0:T(8,128)(2,1)S(1)}, u32[]{:S(2)}) copy-start(bf16[704,2048]{1,0:T(8,128)(2,1)S(1)} %get-tuple-element.15) | copy-start | bytes 8650756
  99.5 4.3 %copy-start.15 = (bf16[8,64,2048]{2,1,0:T(8,128)(2,1)S(1)}, bf16[8,64,2048]{2,1,0:T(8,128)(2,1)}, u32[]{:S(2)}) copy-start(bf16[8,64,2048]{2,1,0:T(8,128)(2,1)} %convolution_convert_fusion.3) | copy-start | bytes 6291460
  103.8 3.9 %copy-start.11 = (bf16[704,2048]{1,0:T(8,128)(2,1)S(1)}, bf16[704,2048]{1,0:T(8,128)(2,1)}, u32[]{:S(2)}) copy-start(bf16[704,2048]{1,0:T(8,128)(2,1)} %get-tuple-element.16) | copy-start | bytes 8650756
  161.7 15.7 %collective-permute-start = (bf16[128,2048]{1,0:T(8,128)(2,1)}, bf16[128,2048]{1,0:T(8,128)(2,1)S(1)}, u32[]{:S(2)}, u32[]{:S(2)}) collective-permute-start(bf16[128,2048]{1,0:T(8,128)(2,1)} %add_convert_fusion.5), channel_id=1, source_target_pairs={{0,1},{2,3},{4,5},{6,7},{8,9},{10,11},{12,13},{14,15},{16,17},{18,... | collective-permute-start | bytes 1572872 | tf_op jit(solution)/shard_map/ppermute | solution.py:297
  178.7 3.8 %copy-start.5 = (bf16[128,2048]{1,0:T(8,128)(2,1)}, bf16[128,2048]{1,0:T(8,128)(2,1)S(1)}, u32[]{:S(2)}) copy-start(bf16[128,2048]{1,0:T(8,128)(2,1)S(1)} %get-tuple-element.14) | copy-start | bytes 1572868
  183.1 4.5 %copy-start.23 = (pred[128,896]{1,0:T(8,128)(4,1)S(1)}, pred[128,896]{1,0:T(8,128)(4,1)}, u32[]{:S(2)}) copy-start(pred[128,896]{1,0:T(8,128)(4,1)} %get-tuple-element.25) | copy-start | bytes 344068
  187.7 6.8 %copy-start.9 = (bf16[768,512]{1,0:T(8,128)(2,1)S(1)}, bf16[768,512]{1,0:T(8,128)(2,1)}, u32[]{:S(2)}) copy-start(bf16[768,512]{1,0:T(8,128)(2,1)} %get-tuple-element.17) | copy-start | bytes 2359300
  187.7 6.8 %copy-start.29 = (bf16[1,8,512,128]{3,2,1,0:T(8,128)(2,1)S(1)}, bf16[1,8,512,128]{3,2,1,0:T(8,128)(2,1)}, u32[]{:S(2)}) copy-start(bf16[1,8,512,128]{3,2,1,0:T(8,128)(2,1)} %param.26) | copy-start | bytes 3145732
  242.0 4.4 %copy-start.2 = (bf16[4,2,128,2048]{3,2,1,0:T(8,128)(2,1)S(1)}, bf16[4,2,128,2048]{3,2,1,0:T(8,128)(2,1)}, u32[]{:S(2)}) copy-start(bf16[4,2,128,2048]{3,2,1,0:T(8,128)(2,1)} %get-tuple-element.12) | copy-start | bytes 12582916
  248.8 4.3 %copy-start.18 = (bf16[8,64,2048]{2,1,0:T(8,128)(2,1)S(1)}, bf16[8,64,2048]{2,1,0:T(8,128)(2,1)}, u32[]{:S(2)}) copy-start(bf16[8,64,2048]{2,1,0:T(8,128)(2,1)} %convolution_convert_fusion) | copy-start | bytes 6291460
  253.1 3.9 %copy-start.14 = (bf16[704,2048]{1,0:T(8,128)(2,1)S(1)}, bf16[704,2048]{1,0:T(8,128)(2,1)}, u32[]{:S(2)}) copy-start(bf16[704,2048]{1,0:T(8,128)(2,1)} %copy-done.13) | copy-start | bytes 8650756
  260.0 4.3 %copy-start.16 = (bf16[8,64,2048]{2,1,0:T(8,128)(2,1)S(1)}, bf16[8,64,2048]{2,1,0:T(8,128)(2,1)}, u32[]{:S(2)}) copy-start(bf16[8,64,2048]{2,1,0:T(8,128)(2,1)} %convolution_convert_fusion.1) | copy-start | bytes 6291460
  264.3 3.9 %copy-start.12 = (bf16[704,2048]{1,0:T(8,128)(2,1)S(1)}, bf16[704,2048]{1,0:T(8,128)(2,1)}, u32[]{:S(2)}) copy-start(bf16[704,2048]{1,0:T(8,128)(2,1)} %get-tuple-element.16) | copy-start | bytes 8650756
  276.7 47.1 %copy-start.1 = (bf16[1,2048,512]{2,1,0:T(8,128)(2,1)S(1)}, bf16[1,2048,512]{2,1,0:T(8,128)(2,1)}, u32[]{:S(2)}) copy-start(bf16[1,2048,512]{2,1,0:T(8,128)(2,1)} %param.28) | copy-start | bytes 6291460
  (7 other events, 15.7 us)

commit v4 on v3

--- a/solution.py
+++ b/solution.py
@@ -152,6 +152,7 @@
     count = lax.axis_size("expert")
     pair = 2 if count % 2 == 0 else 1
     chips = count // pair
+    held = count * own.size * own.dtype.itemsize
     result, small_result = pl.pallas_call(
         spread_kernel,
         out_shape=[
@@ -167,7 +168,10 @@
             pltpu.SemaphoreType.DMA((chips, PIECES + 1)),
             pltpu.SemaphoreType.DMA((chips, PIECES + 1)),
         ],
-        compiler_params=pltpu.CompilerParams(collective_id=0, has_side_effects=True),
+        compiler_params=pltpu.CompilerParams(
+            collective_id=0, has_side_effects=True, vmem_limit_bytes=2 * held
+        ),
+        cost_estimate=pl.CostEstimate(flops=0, bytes_accessed=32 * held, transcendentals=0),
     )(own, small)
     return result.reshape((count,) + own.shape), small_result.reshape((count,) + small.shape)
 
@@ -271,6 +275,7 @@
     count, height, chunk = parts[0].shape
     pieces = len(parts)
     kind = parts[0].dtype
+    held = pieces * parts[0].size * kind.itemsize
     pair = 2 if count % 2 == 0 else 1
     chips = count // pair
     return pl.pallas_call(
@@ -287,7 +292,10 @@
             pltpu.SemaphoreType.DMA((chips, pieces)),
             pltpu.SemaphoreType.DMA((2, chips, pieces)),
         ],
-        compiler_params=pltpu.CompilerParams(collective_id=1, has_side_effects=True),
+        compiler_params=pltpu.CompilerParams(
+            collective_id=1, has_side_effects=True, vmem_limit_bytes=4 * held
+        ),
+        cost_estimate=pl.CostEstimate(flops=0, bytes_accessed=32 * held, transcendentals=0),
     )(*[part.reshape(chips, pair, height, chunk) for part in parts])
 
 

time: 330 us -> 303 us (0.918)
  Pallas kernels: 165 us -> 153 us
  matrix products: 99.6 us -> 89.6 us
    pallas_call x2, Pallas kernels: 87.4 us -> 81.4 us  [gather_sum(): pl.pallas_call(gather_sum_kernel, out_shape=jax.ShapeDtypeStruct((height,...]
    pallas_call x2, Pallas kernels: 78 us -> 72.1 us  [spread(): pl.pallas_call(spread_kernel, out_shape=[jax.ShapeDtypeStruct((chips, pai...]
    dot_general x8, matrix products: 11.9 us -> 6.5 us  [shards(): jnp.einsum('jsr,jsd->jrd', place[:, e], down.reshape(sources, CAP, chunk)...]
    dot_general x4, matrix products: 12.8 us -> 8.13 us  [shards(): jnp.einsum('jsr,jrd->jsd', place[:, e], all_rows, preferred_element_type=...]
where the time goes in v4:
time: 303 us; the launch traced here: 297 us
  Pallas kernels  153 us (50%)
  matrix products  89.6 us (30%)
  other arithmetic  26.7 us (9%)
  waiting for transfers between devices  14.4 us (5%)
  local copies, waits for them, and re-layouts  10.9 us (4%)
    pallas_call x2, Pallas kernels, gather_sum(): pl.pallas_call(gather_sum_kernel, out_shape=jax.ShapeDtypeStruct((height,...  81.4 us
    pallas_call x2, Pallas kernels, spread(): pl.pallas_call(spread_kernel, out_shape=[jax.ShapeDtypeStruct((chips, pai...  72.1 us
    dot_general x4, matrix products, shards(): jnp.dot(rows_in, specialist_switch_factor[0, e], preferred_element_type=j...  17.4 us
    dot_general x4, matrix products, shards(): jnp.dot(rows_in, specialist_widen_factor[0, e], preferred_element_type=jn...  15.3 us
    ppermute x1, waiting for transfers between devices, shifted(): lax.ppermute(value, axis, [(source, source + steps) for source in range(i...  14.4 us
    sub x2, other arithmetic, attend(): expd = jnp.where(visible[:, None, :], jnp.exp(scores - row_max), 0.0)  13.5 us
    dot_general x8, matrix products, shards(): jnp.dot(hidden_list[e], specialist_contract_factor[0, e][:, c * chunk:(c...  11.1 us
    dot_general x2, matrix products, attend(): jnp.einsum('thl,kl->thk', q_lat, key_rows, preferred_element_type=jnp.flo...  9.02 us
  transfers between devices with their start and end apart: 1, of which 1 were waited for; matrix products, arithmetic and copies ran while one was open for 0% of the time, Pallas kernels for 0%

profile of v4, /device:TPU:10, one launch (start us, length us, event | category | flops | bytes accessed | tf_op | source)
XLA Modules:
  0.0 297.2 jit_solution(6589346234186189298)
XLA Ops:
  4.4 3.2 %fusion.130 = bf16[16,8,8,128]{3,2,1,0:T(8,128)(2,1)S(1)} fusion(bf16[1,2048,1024]{2,1,0:T(8,128)(2,1)} %param.24, bf16[1,128,2048]{2,1,0:T(8,128)(2,1)} %param.17, f32[2048]{0:T(1024)} %bitcast.304, f32[128]{0:T(128)S(1)} %add_rsqrt_fusion.5), kind=kOutput, calls=%fused_computation.118 | convolution fusion | flops 538050560 | bytes 4989440 | tf_op jit(solution)/shard_map/dot_general | solution.py:394
  15.1 4.5 %fusion.105 = f32[128,8,896]{2,0,1:T(8,128)} fusion(bf16[1,8,128,512]{3,2,1,0:T(8,128)(2,1)S(1)} %copy-done.5, bf16[128,512]{1,0:T(8,128)(2,1)S(1)} %multiply_convert_fusion.3, bf16[768,512]{1,0:T(8,128)(2,1)} %get-tuple-element.18, bf16[16,8,8,128]{3,2,1,0:T(8,128)(2,1)S(1)} %fusion.130), kind=kOutput, calls=%fused_computation.97 | convolution fusion | flops 1076101120 | bytes 5898240 | tf_op jit(solution)/shard_map/thl,kl->thk/dot_general | solution.py:319
  19.6 6.8 %fusion.192 = (f32[128,8]{0,1:T(8,128)S(1)}, f32[128,8,896]{2,0,1:T(8,128)}) fusion(f32[128,8,896]{2,0,1:T(8,128)} %fusion.105, pred[128,896]{1,0:T(8,128)(4,1)} %get-tuple-element.26), kind=kOutput, calls=%fused_computation.207 | output fusion | flops 6423423 | bytes 7458816 | tf_op jit(solution)/shard_map/sub | solution.py:326
  26.4 3.9 %fusion.126 = bf16[8,128,128]{1,2,0:T(8,128)(2,1)S(1)} fusion(f32[128,8,896]{2,0,1:T(8,128)} %get-tuple-element.32, f32[128,8]{0,1:T(8,128)S(1)} %get-tuple-element.31, bf16[1,8,512,128]{3,2,1,0:T(8,128)(2,1)} %param.26, bf16[128,512]{1,0:T(8,128)(2,1)S(1)} %multiply_convert_fusion.3, bf16[768,512]{1,0:T(8,128)(2,1)S(1)} %copy-done.8), kind=kOutput, calls=%fused_computation.116 | convolution fusion | flops 1078067200 | bytes 5902336 | tf_op jit(solution)/shard_map/thl,hld->thd/dot_general | solution.py:407
  30.4 3.1 %multiply_reduce_fusion.1 = (f32[128]{0:T(128)S(1)}, f32[128,2048]{1,0:T(8,128)S(1)}) fusion(bf16[128,1024]{0,1:T(8,128)(2,1)S(1)} %bitcast.302, bf16[1,1024,2048]{2,1,0:T(8,128)(2,1)} %param.27, bf16[1,128,2048]{2,1,0:T(8,128)(2,1)} %param.17), kind=kOutput, calls=%fused_computation.141 | convolution fusion | flops 538443648 | bytes 6029824 | tf_op jit(solution)/shard_map/dot_general | solution.py:411
  33.7 36.4 %shard_map.163 = (bf16[4,2,128,2048]{3,2,1,0:T(8,128)(2,1)S(1)}, f32[4,2,16,128]{3,2,1,0:T(8,128)S(1)}) custom-call(bf16[128,2048]{1,0:T(8,128)(2,1)S(1)} %multiply_convert_fusion.1.own_ref, f32[16,128]{1,0:T(8,128)S(1)} %get-tuple-element.20.small_ref), custom_call_target="tpu_custom_call" | custom-call | bytes 134217728 | tf_op jit(solution)/shard_map/pallas_call | solution.py:156
  74.9 5.4 %slice_bitcast_fusion = (bf16[704,2048]{1,0:T(8,128)(2,1)S(1)}, bf16[704,2048]{1,0:T(8,128)(2,1)}) fusion(bf16[1,2,704,2048]{3,2,1,0:T(8,128)(2,1)} %param.33), kind=kLoop, calls=%fused_computation.40 | loop fusion | bytes 11534336 | tf_op jit(solution)/shard_map/squeeze | solution.py:460
  80.3 4.5 %fusion.16 = f32[512,704]{0,1:T(8,128)S(1)} fusion(bf16[512,2048]{1,0:T(8,128)(2,1)S(1)} %bitcast.289, bf16[1,2,2048,704]{2,3,1,0:T(8,128)(2,1)} %param.31), kind=kOutput, calls=%fused_computation.30 | convolution fusion | flops 1476395008 | bytes 6422528 | tf_op jit(solution)/shard_map/dot_general | solution.py:442
  84.9 3.7 %fusion.98 = bf16[512,704]{0,1:T(8,128)(2,1)S(1)} fusion(bf16[512,2048]{1,0:T(8,128)(2,1)S(1)} %bitcast.290, bf16[1,2,2048,704]{2,3,1,0:T(8,128)(2,1)} %param.32, f32[512,704]{0,1:T(8,128)S(1)} %fusion.16, f32[512]{0:T(512)S(1)} %mul.222), kind=kOutput, calls=%fused_computation.94 | convolution fusion | flops 1478918144 | bytes 7145472 | tf_op jit(solution)/shard_map/dot_general | solution.py:445
  92.7 4.3 %fusion.24 = f32[512,704]{0,1:T(8,128)S(1)} fusion(bf16[512,2048]{1,0:T(8,128)(2,1)} %bitcast.285, bf16[1,2,2048,704]{2,3,1,0:T(8,128)(2,1)} %param.31), kind=kOutput, calls=%fused_computation.38 | convolution fusion | flops 1476395008 | bytes 6422528 | tf_op jit(solution)/shard_map/dot_general | solution.py:442
  97.0 3.9 %fusion.92 = bf16[512,704]{0,1:T(8,128)(2,1)S(1)} fusion(bf16[512,2048]{1,0:T(8,128)(2,1)S(1)} %bitcast.286, bf16[1,2,2048,704]{2,3,1,0:T(8,128)(2,1)} %param.32, f32[512,704]{0,1:T(8,128)S(1)} %fusion.24, f32[512]{0:T(512)S(1)} %mul.217), kind=kOutput, calls=%fused_computation.92 | convolution fusion | flops 1478918144 | bytes 7145472 | tf_op jit(solution)/shard_map/dot_general | solution.py:445
  107.1 40.7 %shard_map.164 = bf16[128,2048]{1,0:T(8,128)(2,1)S(1)} custom-call(bf16[4,2,128,1024]{3,2,1,0:T(8,128)(2,1)S(1)} %bitcast.279, bf16[4,2,128,1024]{3,2,1,0:T(8,128)(2,1)S(1)} %bitcast.281), custom_call_target="tpu_custom_call" | custom-call | bytes 134217728 | tf_op jit(solution)/shard_map/pallas_call | solution.py:281
  150.0 14.4 %collective-permute-done = bf16[128,2048]{1,0:T(8,128)(2,1)S(1)} collective-permute-done((bf16[128,2048]{1,0:T(8,128)(2,1)}, bf16[128,2048]{1,0:T(8,128)(2,1)S(1)}, u32[]{:S(2)}, u32[]{:S(2)}) %collective-permute-start) | collective-permute-done | bytes 524320 | tf_op jit(solution)/shard_map/ppermute | solution.py:305
  165.8 3.2 %fusion.127 = bf16[16,8,8,128]{3,2,1,0:T(8,128)(2,1)S(1)} fusion(bf16[1,2048,1024]{2,1,0:T(8,128)(2,1)} %param.24, bf16[128,2048]{1,0:T(8,128)(2,1)S(1)} %get-tuple-element.14, f32[2048]{0:T(1024)S(1)} %bitcast.306, f32[128]{0:T(128)S(1)} %add_rsqrt_fusion.2), kind=kOutput, calls=%fused_computation.117 | convolution fusion | flops 538050560 | bytes 4989440 | tf_op jit(solution)/shard_map/dot_general | solution.py:394
  170.2 4.5 %fusion.107 = f32[128,8,896]{2,0,1:T(8,128)} fusion(bf16[1,8,128,512]{3,2,1,0:T(8,128)(2,1)S(1)} %copy-done.6, bf16[128,512]{1,0:T(8,128)(2,1)S(1)} %multiply_convert_fusion.2, bf16[768,512]{1,0:T(8,128)(2,1)} %get-tuple-element.17, bf16[16,8,8,128]{3,2,1,0:T(8,128)(2,1)S(1)} %fusion.127), kind=kOutput, calls=%fused_computation.99 | convolution fusion | flops 1076101120 | bytes 5898240 | tf_op jit(solution)/shard_map/thl,kl->thk/dot_general | solution.py:319
  174.7 6.8 %fusion.193 = (f32[128,8]{0,1:T(8,128)S(1)}, f32[128,8,896]{2,0,1:T(8,128)}) fusion(f32[128,8,896]{2,0,1:T(8,128)} %fusion.107, pred[128,896]{1,0:T(8,128)(4,1)S(1)} %copy-done.21), kind=kOutput, calls=%fused_computation.208 | output fusion | flops 6423423 | bytes 7458816 | tf_op jit(solution)/shard_map/sub | solution.py:326
  181.5 3.7 %fusion.125 = bf16[8,128,128]{1,2,0:T(8,128)(2,1)S(1)} fusion(f32[128,8,896]{2,0,1:T(8,128)} %get-tuple-element.38, f32[128,8]{0,1:T(8,128)S(1)} %get-tuple-element.37, bf16[1,8,512,128]{3,2,1,0:T(8,128)(2,1)S(1)} %copy-done.28, bf16[128,512]{1,0:T(8,128)(2,1)S(1)} %multiply_convert_fusion.2, bf16[768,512]{1,0:T(8,128)(2,1)S(1)} %copy-done.7), kind=kOutput, calls=%fused_computation.115 | convolution fusion | flops 1078067200 | bytes 5902336 | tf_op jit(solution)/shard_map/thl,hld->thd/dot_general | solution.py:407
  185.2 3.0 %multiply_reduce_fusion = (f32[128]{0:T(128)S(1)}, f32[128,2048]{1,0:T(8,128)S(1)}) fusion(bf16[128,1024]{0,1:T(8,128)(2,1)S(1)} %bitcast.301, bf16[1,1024,2048]{2,1,0:T(8,128)(2,1)} %param.27, bf16[128,2048]{1,0:T(8,128)(2,1)S(1)} %copy-done.4), kind=kOutput, calls=%fused_computation.138 | convolution fusion | flops 538443648 | bytes 6029824 | tf_op jit(solution)/shard_map/dot_general | solution.py:411
  188.4 35.8 %shard_map.165 = (bf16[4,2,128,2048]{3,2,1,0:T(8,128)(2,1)S(1)}, f32[4,2,16,128]{3,2,1,0:T(8,128)S(1)}) custom-call(bf16[128,2048]{1,0:T(8,128)(2,1)S(1)} %multiply_convert_fusion.own_ref, f32[16,128]{1,0:T(8,128)S(1)} %get-tuple-element.19.small_ref), custom_call_target="tpu_custom_call" | custom-call | bytes 134217728 | tf_op jit(solution)/shard_map/pallas_call | solution.py:156
  229.0 4.3 %fusion.14 = f32[512,704]{0,1:T(8,128)S(1)} fusion(bf16[512,2048]{1,0:T(8,128)(2,1)} %bitcast.291, bf16[1,2,2048,704]{2,3,1,0:T(8,128)(2,1)} %param.31), kind=kOutput, calls=%fused_computation.28 | convolution fusion | flops 1476395008 | bytes 6422528 | tf_op jit(solution)/shard_map/dot_general | solution.py:442
  233.3 3.9 %fusion.101 = bf16[512,704]{0,1:T(8,128)(2,1)S(1)} fusion(bf16[512,2048]{1,0:T(8,128)(2,1)S(1)} %bitcast.292, bf16[1,2,2048,704]{2,3,1,0:T(8,128)(2,1)} %param.32, f32[512,704]{0,1:T(8,128)S(1)} %fusion.14, f32[512]{0:T(512)S(1)} %mul.246), kind=kOutput, calls=%fused_computation.95 | convolution fusion | flops 1478918144 | bytes 7145472 | tf_op jit(solution)/shard_map/dot_general | solution.py:445
  240.3 4.3 %fusion.22 = f32[512,704]{0,1:T(8,128)S(1)} fusion(bf16[512,2048]{1,0:T(8,128)(2,1)} %bitcast.287, bf16[1,2,2048,704]{2,3,1,0:T(8,128)(2,1)} %param.31), kind=kOutput, calls=%fused_computation.36 | convolution fusion | flops 1476395008 | bytes 6422528 | tf_op jit(solution)/shard_map/dot_general | solution.py:442
  244.6 3.9 %fusion.95 = bf16[512,704]{0,1:T(8,128)(2,1)S(1)} fusion(bf16[512,2048]{1,0:T(8,128)(2,1)S(1)} %bitcast.288, bf16[1,2,2048,704]{2,3,1,0:T(8,128)(2,1)} %param.32, f32[512,704]{0,1:T(8,128)S(1)} %fusion.22, f32[512]{0:T(512)S(1)} %mul.241), kind=kOutput, calls=%fused_computation.93 | convolution fusion | flops 1478918144 | bytes 7145472 | tf_op jit(solution)/shard_map/dot_general | solution.py:445
  254.0 40.7 %shard_map.166 = bf16[128,2048]{1,0:T(8,128)(2,1)S(1)} custom-call(bf16[4,2,128,1024]{3,2,1,0:T(8,128)(2,1)S(1)} %bitcast.282, bf16[4,2,128,1024]{3,2,1,0:T(8,128)(2,1)S(1)} %bitcast.280), custom_call_target="tpu_custom_call" | custom-call | bytes 134217728 | tf_op jit(solution)/shard_map/pallas_call | solution.py:281
  (127 shorter events, 47.6 us)
Async XLA Ops:
  0.0 7.6 %copy-start = (bf16[1,2048,512]{2,1,0:T(8,128)(2,1)S(1)}, bf16[1,2048,512]{2,1,0:T(8,128)(2,1)}, u32[]{:S(2)}) copy-start(bf16[1,2048,512]{2,1,0:T(8,128)(2,1)} %param.28) | copy-start | bytes 6291460
  0.0 7.7 %copy-start.2 = (bf16[1,128,2048]{2,1,0:T(8,128)(2,1)S(1)}, bf16[1,128,2048]{2,1,0:T(8,128)(2,1)}, u32[]{:S(2)}) copy-start(bf16[1,128,2048]{2,1,0:T(8,128)(2,1)} %param.17) | copy-start | bytes 1572868
  0.0 7.7 %copy-start.22 = (f32[1,2048]{1,0:T(1,128)S(1)}, f32[1,2048]{1,0:T(1,128)}, u32[]{:S(2)}) copy-start(f32[1,2048]{1,0:T(1,128)} %param.23) | copy-start | bytes 24580
  4.4 5.1 %copy-start.17 = (bf16[2,1,1,768,512]{4,3,2,1,0:T(8,128)(2,1)S(1)}, bf16[2,1,1,768,512]{4,3,2,1,0:T(8,128)(2,1)}, u32[]{:S(2)}) copy-start(bf16[2,1,1,768,512]{4,3,2,1,0:T(8,128)(2,1)} %param.19) | copy-start | bytes 4718596
  8.9 6.3 %copy-start.5 = (bf16[1,8,128,512]{3,2,1,0:T(8,128)(2,1)S(1)}, bf16[1,8,128,512]{3,2,1,0:T(8,128)(2,1)}, u32[]{:S(2)}) copy-start(bf16[1,8,128,512]{3,2,1,0:T(8,128)(2,1)} %param.25) | copy-start | bytes 3145732
  19.6 6.8 %copy-start.8 = (bf16[768,512]{1,0:T(8,128)(2,1)S(1)}, bf16[768,512]{1,0:T(8,128)(2,1)}, u32[]{:S(2)}) copy-start(bf16[768,512]{1,0:T(8,128)(2,1)} %get-tuple-element.18) | copy-start | bytes 2359300
  30.4 39.9 %copy-start.26 = (s32[64]{0:T(128)S(1)}, s32[64]{0:T(128)}, u32[]{:S(2)}) copy-start(s32[64]{0:T(128)} %iota_add_fusion.1) | copy-start | bytes 772
  74.9 5.5 %copy-start.15 = (bf16[8,64,2048]{2,1,0:T(8,128)(2,1)S(1)}, bf16[8,64,2048]{2,1,0:T(8,128)(2,1)}, u32[]{:S(2)}) copy-start(bf16[8,64,2048]{2,1,0:T(8,128)(2,1)} %convolution_convert_fusion.2) | copy-start | bytes 6291460
  80.3 10.3 %copy-start.11 = (bf16[704,2048]{1,0:T(8,128)(2,1)}, bf16[704,2048]{1,0:T(8,128)(2,1)S(1)}, u32[]{:S(2)}) copy-start(bf16[704,2048]{1,0:T(8,128)(2,1)S(1)} %get-tuple-element.15) | copy-start | bytes 8650756
  92.6 4.3 %copy-start.13 = (bf16[8,64,2048]{2,1,0:T(8,128)(2,1)S(1)}, bf16[8,64,2048]{2,1,0:T(8,128)(2,1)}, u32[]{:S(2)}) copy-start(bf16[8,64,2048]{2,1,0:T(8,128)(2,1)} %convolution_convert_fusion.3) | copy-start | bytes 6291460
  96.9 3.9 %copy-start.9 = (bf16[704,2048]{1,0:T(8,128)(2,1)S(1)}, bf16[704,2048]{1,0:T(8,128)(2,1)}, u32[]{:S(2)}) copy-start(bf16[704,2048]{1,0:T(8,128)(2,1)} %get-tuple-element.16) | copy-start | bytes 8650756
  147.8 18.0 %copy-start.23 = (f32[1,2048]{1,0:T(1,128)S(1)}, f32[1,2048]{1,0:T(1,128)}, u32[]{:S(2)}) copy-start(f32[1,2048]{1,0:T(1,128)} %param.23) | copy-start | bytes 24580
  148.7 15.7 %collective-permute-start = (bf16[128,2048]{1,0:T(8,128)(2,1)}, bf16[128,2048]{1,0:T(8,128)(2,1)S(1)}, u32[]{:S(2)}, u32[]{:S(2)}) collective-permute-start(bf16[128,2048]{1,0:T(8,128)(2,1)} %add_convert_fusion.5), channel_id=1, source_target_pairs={{0,1},{2,3},{4,5},{6,7},{8,9},{10,11},{12,13},{14,15},{16,17},{18,... | collective-permute-start | bytes 1572872 | tf_op jit(solution)/shard_map/ppermute | solution.py:305
  165.7 3.8 %copy-start.3 = (bf16[128,2048]{1,0:T(8,128)(2,1)}, bf16[128,2048]{1,0:T(8,128)(2,1)S(1)}, u32[]{:S(2)}) copy-start(bf16[128,2048]{1,0:T(8,128)(2,1)S(1)} %get-tuple-element.14) | copy-start | bytes 1572868
  165.8 3.8 %copy-start.25 = (f32[1,512]{1,0:T(1,128)S(1)}, f32[1,512]{1,0:T(1,128)}, u32[]{:S(2)}) copy-start(f32[1,512]{1,0:T(1,128)} %param.29) | copy-start | bytes 6148
  170.2 4.5 %copy-start.21 = (pred[128,896]{1,0:T(8,128)(4,1)S(1)}, pred[128,896]{1,0:T(8,128)(4,1)}, u32[]{:S(2)}) copy-start(pred[128,896]{1,0:T(8,128)(4,1)} %get-tuple-element.25) | copy-start | bytes 344068
  174.7 6.8 %copy-start.7 = (bf16[768,512]{1,0:T(8,128)(2,1)S(1)}, bf16[768,512]{1,0:T(8,128)(2,1)}, u32[]{:S(2)}) copy-start(bf16[768,512]{1,0:T(8,128)(2,1)} %get-tuple-element.17) | copy-start | bytes 2359300
  174.7 6.8 %copy-start.28 = (bf16[1,8,512,128]{3,2,1,0:T(8,128)(2,1)S(1)}, bf16[1,8,512,128]{3,2,1,0:T(8,128)(2,1)}, u32[]{:S(2)}) copy-start(bf16[1,8,512,128]{3,2,1,0:T(8,128)(2,1)} %param.26) | copy-start | bytes 3145732
  181.5 3.7 %copy-start.4 = (bf16[128,2048]{1,0:T(8,128)(2,1)S(1)}, bf16[128,2048]{1,0:T(8,128)(2,1)}, u32[]{:S(2)}) copy-start(bf16[128,2048]{1,0:T(8,128)(2,1)} %copy-done.3) | copy-start | bytes 1572868
  229.0 4.3 %copy-start.16 = (bf16[8,64,2048]{2,1,0:T(8,128)(2,1)S(1)}, bf16[8,64,2048]{2,1,0:T(8,128)(2,1)}, u32[]{:S(2)}) copy-start(bf16[8,64,2048]{2,1,0:T(8,128)(2,1)} %convolution_convert_fusion) | copy-start | bytes 6291460
  233.3 3.9 %copy-start.12 = (bf16[704,2048]{1,0:T(8,128)(2,1)S(1)}, bf16[704,2048]{1,0:T(8,128)(2,1)}, u32[]{:S(2)}) copy-start(bf16[704,2048]{1,0:T(8,128)(2,1)} %copy-done.11) | copy-start | bytes 8650756
  240.3 4.3 %copy-start.14 = (bf16[8,64,2048]{2,1,0:T(8,128)(2,1)S(1)}, bf16[8,64,2048]{2,1,0:T(8,128)(2,1)}, u32[]{:S(2)}) copy-start(bf16[8,64,2048]{2,1,0:T(8,128)(2,1)} %convolution_convert_fusion.1) | copy-start | bytes 6291460
  244.6 3.9 %copy-start.10 = (bf16[704,2048]{1,0:T(8,128)(2,1)S(1)}, bf16[704,2048]{1,0:T(8,128)(2,1)}, u32[]{:S(2)}) copy-start(bf16[704,2048]{1,0:T(8,128)(2,1)} %get-tuple-element.16) | copy-start | bytes 8650756
  254.0 43.0 %copy-start.1 = (bf16[1,2048,512]{2,1,0:T(8,128)(2,1)S(1)}, bf16[1,2048,512]{2,1,0:T(8,128)(2,1)}, u32[]{:S(2)}) copy-start(bf16[1,2048,512]{2,1,0:T(8,128)(2,1)} %param.28) | copy-start | bytes 6291460
  (6 other events, 11.1 us)

commit v5 on v4

--- a/solution.py
+++ b/solution.py
@@ -13,7 +13,7 @@
 
 
 MESH = pl.DeviceIdType.MESH
-PIECES = 2
+PIECES = 4
 
 
 def place_on_line():

time: 303 us -> 304 us (level)
  no operation moved by 1% of the time
where the time goes in v5:
time: 304 us; the launch traced here: 298 us
  Pallas kernels  154 us (51%)
  matrix products  89.7 us (30%)
  other arithmetic  26.7 us (9%)
  waiting for transfers between devices  14.4 us (5%)
  local copies, waits for them, and re-layouts  11 us (4%)
    pallas_call x2, Pallas kernels, gather_sum(): pl.pallas_call(gather_sum_kernel, out_shape=jax.ShapeDtypeStruct((height,...  81 us
    pallas_call x2, Pallas kernels, spread(): pl.pallas_call(spread_kernel, out_shape=[jax.ShapeDtypeStruct((chips, pai...  72.8 us
    dot_general x4, matrix products, shards(): jnp.dot(rows_in, specialist_switch_factor[0, e], preferred_element_type=j...  17.4 us
    dot_general x4, matrix products, shards(): jnp.dot(rows_in, specialist_widen_factor[0, e], preferred_element_type=jn...  15.3 us
    ppermute x1, waiting for transfers between devices, shifted(): lax.ppermute(value, axis, [(source, source + steps) for source in range(i...  14.4 us
    sub x2, other arithmetic, attend(): expd = jnp.where(visible[:, None, :], jnp.exp(scores - row_max), 0.0)  13.5 us
    dot_general x8, matrix products, shards(): jnp.dot(hidden_list[e], specialist_contract_factor[0, e][:, c * chunk:(c...  11.3 us
    dot_general x2, matrix products, attend(): jnp.einsum('thl,kl->thk', q_lat, key_rows, preferred_element_type=jnp.flo...  9.02 us
  transfers between devices with their start and end apart: 1, of which 1 were waited for; matrix products, arithmetic and copies ran while one was open for 0% of the time, Pallas kernels for 0%

profile of v5, /device:TPU:10, one launch (start us, length us, event | category | flops | bytes accessed | tf_op | source)
XLA Modules:
  0.0 297.7 jit_solution(4993022010774212078)
XLA Ops:
  4.4 3.2 %fusion.130 = bf16[16,8,8,128]{3,2,1,0:T(8,128)(2,1)S(1)} fusion(bf16[1,2048,1024]{2,1,0:T(8,128)(2,1)} %param.24, bf16[1,128,2048]{2,1,0:T(8,128)(2,1)} %param.17, f32[2048]{0:T(1024)} %bitcast.304, f32[128]{0:T(128)S(1)} %add_rsqrt_fusion.5), kind=kOutput, calls=%fused_computation.118 | convolution fusion | flops 538050560 | bytes 4989440 | tf_op jit(solution)/shard_map/dot_general | solution.py:394
  15.1 4.5 %fusion.105 = f32[128,8,896]{2,0,1:T(8,128)} fusion(bf16[1,8,128,512]{3,2,1,0:T(8,128)(2,1)S(1)} %copy-done.5, bf16[128,512]{1,0:T(8,128)(2,1)S(1)} %multiply_convert_fusion.3, bf16[768,512]{1,0:T(8,128)(2,1)} %get-tuple-element.18, bf16[16,8,8,128]{3,2,1,0:T(8,128)(2,1)S(1)} %fusion.130), kind=kOutput, calls=%fused_computation.97 | convolution fusion | flops 1076101120 | bytes 5898240 | tf_op jit(solution)/shard_map/thl,kl->thk/dot_general | solution.py:319
  19.6 6.8 %fusion.192 = (f32[128,8]{0,1:T(8,128)S(1)}, f32[128,8,896]{2,0,1:T(8,128)}) fusion(f32[128,8,896]{2,0,1:T(8,128)} %fusion.105, pred[128,896]{1,0:T(8,128)(4,1)} %get-tuple-element.26), kind=kOutput, calls=%fused_computation.207 | output fusion | flops 6423423 | bytes 7458816 | tf_op jit(solution)/shard_map/sub | solution.py:326
  26.4 3.9 %fusion.126 = bf16[8,128,128]{1,2,0:T(8,128)(2,1)S(1)} fusion(f32[128,8,896]{2,0,1:T(8,128)} %get-tuple-element.32, f32[128,8]{0,1:T(8,128)S(1)} %get-tuple-element.31, bf16[1,8,512,128]{3,2,1,0:T(8,128)(2,1)} %param.26, bf16[128,512]{1,0:T(8,128)(2,1)S(1)} %multiply_convert_fusion.3, bf16[768,512]{1,0:T(8,128)(2,1)S(1)} %copy-done.8), kind=kOutput, calls=%fused_computation.116 | convolution fusion | flops 1078067200 | bytes 5902336 | tf_op jit(solution)/shard_map/thl,hld->thd/dot_general | solution.py:407
  30.4 3.1 %multiply_reduce_fusion.1 = (f32[128]{0:T(128)S(1)}, f32[128,2048]{1,0:T(8,128)S(1)}) fusion(bf16[128,1024]{0,1:T(8,128)(2,1)S(1)} %bitcast.302, bf16[1,1024,2048]{2,1,0:T(8,128)(2,1)} %param.27, bf16[1,128,2048]{2,1,0:T(8,128)(2,1)} %param.17), kind=kOutput, calls=%fused_computation.141 | convolution fusion | flops 538443648 | bytes 6029824 | tf_op jit(solution)/shard_map/dot_general | solution.py:411
  33.7 36.7 %shard_map.163 = (bf16[4,2,128,2048]{3,2,1,0:T(8,128)(2,1)S(1)}, f32[4,2,16,128]{3,2,1,0:T(8,128)S(1)}) custom-call(bf16[128,2048]{1,0:T(8,128)(2,1)S(1)} %multiply_convert_fusion.1.own_ref, f32[16,128]{1,0:T(8,128)S(1)} %get-tuple-element.20.small_ref), custom_call_target="tpu_custom_call" | custom-call | bytes 134217728 | tf_op jit(solution)/shard_map/pallas_call | solution.py:156
  75.2 5.4 %slice_bitcast_fusion = (bf16[704,2048]{1,0:T(8,128)(2,1)S(1)}, bf16[704,2048]{1,0:T(8,128)(2,1)}) fusion(bf16[1,2,704,2048]{3,2,1,0:T(8,128)(2,1)} %param.33), kind=kLoop, calls=%fused_computation.40 | loop fusion | bytes 11534336 | tf_op jit(solution)/shard_map/squeeze | solution.py:460
  80.7 4.5 %fusion.16 = f32[512,704]{0,1:T(8,128)S(1)} fusion(bf16[512,2048]{1,0:T(8,128)(2,1)S(1)} %bitcast.289, bf16[1,2,2048,704]{2,3,1,0:T(8,128)(2,1)} %param.31), kind=kOutput, calls=%fused_computation.30 | convolution fusion | flops 1476395008 | bytes 6422528 | tf_op jit(solution)/shard_map/dot_general | solution.py:442
  85.2 3.7 %fusion.98 = bf16[512,704]{0,1:T(8,128)(2,1)S(1)} fusion(bf16[512,2048]{1,0:T(8,128)(2,1)S(1)} %bitcast.290, bf16[1,2,2048,704]{2,3,1,0:T(8,128)(2,1)} %param.32, f32[512,704]{0,1:T(8,128)S(1)} %fusion.16, f32[512]{0:T(512)S(1)} %mul.222), kind=kOutput, calls=%fused_computation.94 | convolution fusion | flops 1478918144 | bytes 7145472 | tf_op jit(solution)/shard_map/dot_general | solution.py:445
  93.0 4.3 %fusion.24 = f32[512,704]{0,1:T(8,128)S(1)} fusion(bf16[512,2048]{1,0:T(8,128)(2,1)} %bitcast.285, bf16[1,2,2048,704]{2,3,1,0:T(8,128)(2,1)} %param.31), kind=kOutput, calls=%fused_computation.38 | convolution fusion | flops 1476395008 | bytes 6422528 | tf_op jit(solution)/shard_map/dot_general | solution.py:442
  97.3 3.9 %fusion.92 = bf16[512,704]{0,1:T(8,128)(2,1)S(1)} fusion(bf16[512,2048]{1,0:T(8,128)(2,1)S(1)} %bitcast.286, bf16[1,2,2048,704]{2,3,1,0:T(8,128)(2,1)} %param.32, f32[512,704]{0,1:T(8,128)S(1)} %fusion.24, f32[512]{0:T(512)S(1)} %mul.217), kind=kOutput, calls=%fused_computation.92 | convolution fusion | flops 1478918144 | bytes 7145472 | tf_op jit(solution)/shard_map/dot_general | solution.py:445
  107.4 40.5 %shard_map.164 = bf16[128,2048]{1,0:T(8,128)(2,1)S(1)} custom-call(bf16[4,2,128,1024]{3,2,1,0:T(8,128)(2,1)S(1)} %bitcast.279, bf16[4,2,128,1024]{3,2,1,0:T(8,128)(2,1)S(1)} %bitcast.281), custom_call_target="tpu_custom_call" | custom-call | bytes 134217728 | tf_op jit(solution)/shard_map/pallas_call | solution.py:281
  150.2 14.4 %collective-permute-done = bf16[128,2048]{1,0:T(8,128)(2,1)S(1)} collective-permute-done((bf16[128,2048]{1,0:T(8,128)(2,1)}, bf16[128,2048]{1,0:T(8,128)(2,1)S(1)}, u32[]{:S(2)}, u32[]{:S(2)}) %collective-permute-start) | collective-permute-done | bytes 524320 | tf_op jit(solution)/shard_map/ppermute | solution.py:305
  166.0 3.2 %fusion.127 = bf16[16,8,8,128]{3,2,1,0:T(8,128)(2,1)S(1)} fusion(bf16[1,2048,1024]{2,1,0:T(8,128)(2,1)} %param.24, bf16[128,2048]{1,0:T(8,128)(2,1)S(1)} %get-tuple-element.14, f32[2048]{0:T(1024)S(1)} %bitcast.306, f32[128]{0:T(128)S(1)} %add_rsqrt_fusion.2), kind=kOutput, calls=%fused_computation.117 | convolution fusion | flops 538050560 | bytes 4989440 | tf_op jit(solution)/shard_map/dot_general | solution.py:394
  170.4 4.5 %fusion.107 = f32[128,8,896]{2,0,1:T(8,128)} fusion(bf16[1,8,128,512]{3,2,1,0:T(8,128)(2,1)S(1)} %copy-done.6, bf16[128,512]{1,0:T(8,128)(2,1)S(1)} %multiply_convert_fusion.2, bf16[768,512]{1,0:T(8,128)(2,1)} %get-tuple-element.17, bf16[16,8,8,128]{3,2,1,0:T(8,128)(2,1)S(1)} %fusion.127), kind=kOutput, calls=%fused_computation.99 | convolution fusion | flops 1076101120 | bytes 5898240 | tf_op jit(solution)/shard_map/thl,kl->thk/dot_general | solution.py:319
  174.9 6.8 %fusion.193 = (f32[128,8]{0,1:T(8,128)S(1)}, f32[128,8,896]{2,0,1:T(8,128)}) fusion(f32[128,8,896]{2,0,1:T(8,128)} %fusion.107, pred[128,896]{1,0:T(8,128)(4,1)S(1)} %copy-done.21), kind=kOutput, calls=%fused_computation.208 | output fusion | flops 6423423 | bytes 7458816 | tf_op jit(solution)/shard_map/sub | solution.py:326
  181.7 3.7 %fusion.125 = bf16[8,128,128]{1,2,0:T(8,128)(2,1)S(1)} fusion(f32[128,8,896]{2,0,1:T(8,128)} %get-tuple-element.38, f32[128,8]{0,1:T(8,128)S(1)} %get-tuple-element.37, bf16[1,8,512,128]{3,2,1,0:T(8,128)(2,1)S(1)} %copy-done.28, bf16[128,512]{1,0:T(8,128)(2,1)S(1)} %multiply_convert_fusion.2, bf16[768,512]{1,0:T(8,128)(2,1)S(1)} %copy-done.7), kind=kOutput, calls=%fused_computation.115 | convolution fusion | flops 1078067200 | bytes 5902336 | tf_op jit(solution)/shard_map/thl,hld->thd/dot_general | solution.py:407
  185.4 3.0 %multiply_reduce_fusion = (f32[128]{0:T(128)S(1)}, f32[128,2048]{1,0:T(8,128)S(1)}) fusion(bf16[128,1024]{0,1:T(8,128)(2,1)S(1)} %bitcast.301, bf16[1,1024,2048]{2,1,0:T(8,128)(2,1)} %param.27, bf16[128,2048]{1,0:T(8,128)(2,1)S(1)} %copy-done.4), kind=kOutput, calls=%fused_computation.138 | convolution fusion | flops 538443648 | bytes 6029824 | tf_op jit(solution)/shard_map/dot_general | solution.py:411
  188.6 36.1 %shard_map.165 = (bf16[4,2,128,2048]{3,2,1,0:T(8,128)(2,1)S(1)}, f32[4,2,16,128]{3,2,1,0:T(8,128)S(1)}) custom-call(bf16[128,2048]{1,0:T(8,128)(2,1)S(1)} %multiply_convert_fusion.own_ref, f32[16,128]{1,0:T(8,128)S(1)} %get-tuple-element.19.small_ref), custom_call_target="tpu_custom_call" | custom-call | bytes 134217728 | tf_op jit(solution)/shard_map/pallas_call | solution.py:156
  229.5 4.3 %fusion.14 = f32[512,704]{0,1:T(8,128)S(1)} fusion(bf16[512,2048]{1,0:T(8,128)(2,1)} %bitcast.291, bf16[1,2,2048,704]{2,3,1,0:T(8,128)(2,1)} %param.31), kind=kOutput, calls=%fused_computation.28 | convolution fusion | flops 1476395008 | bytes 6422528 | tf_op jit(solution)/shard_map/dot_general | solution.py:442
  233.9 3.9 %fusion.101 = bf16[512,704]{0,1:T(8,128)(2,1)S(1)} fusion(bf16[512,2048]{1,0:T(8,128)(2,1)S(1)} %bitcast.292, bf16[1,2,2048,704]{2,3,1,0:T(8,128)(2,1)} %param.32, f32[512,704]{0,1:T(8,128)S(1)} %fusion.14, f32[512]{0:T(512)S(1)} %mul.246), kind=kOutput, calls=%fused_computation.95 | convolution fusion | flops 1478918144 | bytes 7145472 | tf_op jit(solution)/shard_map/dot_general | solution.py:445
  240.8 4.3 %fusion.22 = f32[512,704]{0,1:T(8,128)S(1)} fusion(bf16[512,2048]{1,0:T(8,128)(2,1)} %bitcast.287, bf16[1,2,2048,704]{2,3,1,0:T(8,128)(2,1)} %param.31), kind=kOutput, calls=%fused_computation.36 | convolution fusion | flops 1476395008 | bytes 6422528 | tf_op jit(solution)/shard_map/dot_general | solution.py:442
  245.1 3.9 %fusion.95 = bf16[512,704]{0,1:T(8,128)(2,1)S(1)} fusion(bf16[512,2048]{1,0:T(8,128)(2,1)S(1)} %bitcast.288, bf16[1,2,2048,704]{2,3,1,0:T(8,128)(2,1)} %param.32, f32[512,704]{0,1:T(8,128)S(1)} %fusion.22, f32[512]{0:T(512)S(1)} %mul.241), kind=kOutput, calls=%fused_computation.93 | convolution fusion | flops 1478918144 | bytes 7145472 | tf_op jit(solution)/shard_map/dot_general | solution.py:445
  254.8 40.5 %shard_map.166 = bf16[128,2048]{1,0:T(8,128)(2,1)S(1)} custom-call(bf16[4,2,128,1024]{3,2,1,0:T(8,128)(2,1)S(1)} %bitcast.282, bf16[4,2,128,1024]{3,2,1,0:T(8,128)(2,1)S(1)} %bitcast.280), custom_call_target="tpu_custom_call" | custom-call | bytes 134217728 | tf_op jit(solution)/shard_map/pallas_call | solution.py:281
  (127 shorter events, 47.8 us)
Async XLA Ops:
  0.0 7.6 %copy-start = (bf16[1,2048,512]{2,1,0:T(8,128)(2,1)S(1)}, bf16[1,2048,512]{2,1,0:T(8,128)(2,1)}, u32[]{:S(2)}) copy-start(bf16[1,2048,512]{2,1,0:T(8,128)(2,1)} %param.28) | copy-start | bytes 6291460
  0.0 7.7 %copy-start.2 = (bf16[1,128,2048]{2,1,0:T(8,128)(2,1)S(1)}, bf16[1,128,2048]{2,1,0:T(8,128)(2,1)}, u32[]{:S(2)}) copy-start(bf16[1,128,2048]{2,1,0:T(8,128)(2,1)} %param.17) | copy-start | bytes 1572868
  0.0 7.7 %copy-start.22 = (f32[1,2048]{1,0:T(1,128)S(1)}, f32[1,2048]{1,0:T(1,128)}, u32[]{:S(2)}) copy-start(f32[1,2048]{1,0:T(1,128)} %param.23) | copy-start | bytes 24580
  4.4 5.1 %copy-start.17 = (bf16[2,1,1,768,512]{4,3,2,1,0:T(8,128)(2,1)S(1)}, bf16[2,1,1,768,512]{4,3,2,1,0:T(8,128)(2,1)}, u32[]{:S(2)}) copy-start(bf16[2,1,1,768,512]{4,3,2,1,0:T(8,128)(2,1)} %param.19) | copy-start | bytes 4718596
  8.9 6.3 %copy-start.5 = (bf16[1,8,128,512]{3,2,1,0:T(8,128)(2,1)S(1)}, bf16[1,8,128,512]{3,2,1,0:T(8,128)(2,1)}, u32[]{:S(2)}) copy-start(bf16[1,8,128,512]{3,2,1,0:T(8,128)(2,1)} %param.25) | copy-start | bytes 3145732
  19.6 6.8 %copy-start.8 = (bf16[768,512]{1,0:T(8,128)(2,1)S(1)}, bf16[768,512]{1,0:T(8,128)(2,1)}, u32[]{:S(2)}) copy-start(bf16[768,512]{1,0:T(8,128)(2,1)} %get-tuple-element.18) | copy-start | bytes 2359300
  30.4 40.2 %copy-start.26 = (s32[64]{0:T(128)S(1)}, s32[64]{0:T(128)}, u32[]{:S(2)}) copy-start(s32[64]{0:T(128)} %iota_add_fusion.1) | copy-start | bytes 772
  75.2 5.5 %copy-start.15 = (bf16[8,64,2048]{2,1,0:T(8,128)(2,1)S(1)}, bf16[8,64,2048]{2,1,0:T(8,128)(2,1)}, u32[]{:S(2)}) copy-start(bf16[8,64,2048]{2,1,0:T(8,128)(2,1)} %convolution_convert_fusion.2) | copy-start | bytes 6291460
  80.7 10.3 %copy-start.11 = (bf16[704,2048]{1,0:T(8,128)(2,1)}, bf16[704,2048]{1,0:T(8,128)(2,1)S(1)}, u32[]{:S(2)}) copy-start(bf16[704,2048]{1,0:T(8,128)(2,1)S(1)} %get-tuple-element.15) | copy-start | bytes 8650756
  93.0 4.3 %copy-start.13 = (bf16[8,64,2048]{2,1,0:T(8,128)(2,1)S(1)}, bf16[8,64,2048]{2,1,0:T(8,128)(2,1)}, u32[]{:S(2)}) copy-start(bf16[8,64,2048]{2,1,0:T(8,128)(2,1)} %convolution_convert_fusion.3) | copy-start | bytes 6291460
  97.3 3.9 %copy-start.9 = (bf16[704,2048]{1,0:T(8,128)(2,1)S(1)}, bf16[704,2048]{1,0:T(8,128)(2,1)}, u32[]{:S(2)}) copy-start(bf16[704,2048]{1,0:T(8,128)(2,1)} %get-tuple-element.16) | copy-start | bytes 8650756
  147.9 18.0 %copy-start.23 = (f32[1,2048]{1,0:T(1,128)S(1)}, f32[1,2048]{1,0:T(1,128)}, u32[]{:S(2)}) copy-start(f32[1,2048]{1,0:T(1,128)} %param.23) | copy-start | bytes 24580
  148.9 15.7 %collective-permute-start = (bf16[128,2048]{1,0:T(8,128)(2,1)}, bf16[128,2048]{1,0:T(8,128)(2,1)S(1)}, u32[]{:S(2)}, u32[]{:S(2)}) collective-permute-start(bf16[128,2048]{1,0:T(8,128)(2,1)} %add_convert_fusion.5), channel_id=1, source_target_pairs={{0,1},{2,3},{4,5},{6,7},{8,9},{10,11},{12,13},{14,15},{16,17},{18,... | collective-permute-start | bytes 1572872 | tf_op jit(solution)/shard_map/ppermute | solution.py:305
  165.9 3.8 %copy-start.3 = (bf16[128,2048]{1,0:T(8,128)(2,1)}, bf16[128,2048]{1,0:T(8,128)(2,1)S(1)}, u32[]{:S(2)}) copy-start(bf16[128,2048]{1,0:T(8,128)(2,1)S(1)} %get-tuple-element.14) | copy-start | bytes 1572868
  166.0 3.8 %copy-start.25 = (f32[1,512]{1,0:T(1,128)S(1)}, f32[1,512]{1,0:T(1,128)}, u32[]{:S(2)}) copy-start(f32[1,512]{1,0:T(1,128)} %param.29) | copy-start | bytes 6148
  170.4 4.5 %copy-start.21 = (pred[128,896]{1,0:T(8,128)(4,1)S(1)}, pred[128,896]{1,0:T(8,128)(4,1)}, u32[]{:S(2)}) copy-start(pred[128,896]{1,0:T(8,128)(4,1)} %get-tuple-element.25) | copy-start | bytes 344068
  174.9 6.8 %copy-start.7 = (bf16[768,512]{1,0:T(8,128)(2,1)S(1)}, bf16[768,512]{1,0:T(8,128)(2,1)}, u32[]{:S(2)}) copy-start(bf16[768,512]{1,0:T(8,128)(2,1)} %get-tuple-element.17) | copy-start | bytes 2359300
  174.9 6.8 %copy-start.28 = (bf16[1,8,512,128]{3,2,1,0:T(8,128)(2,1)S(1)}, bf16[1,8,512,128]{3,2,1,0:T(8,128)(2,1)}, u32[]{:S(2)}) copy-start(bf16[1,8,512,128]{3,2,1,0:T(8,128)(2,1)} %param.26) | copy-start | bytes 3145732
  181.7 3.7 %copy-start.4 = (bf16[128,2048]{1,0:T(8,128)(2,1)S(1)}, bf16[128,2048]{1,0:T(8,128)(2,1)}, u32[]{:S(2)}) copy-start(bf16[128,2048]{1,0:T(8,128)(2,1)} %copy-done.3) | copy-start | bytes 1572868
  229.5 4.3 %copy-start.16 = (bf16[8,64,2048]{2,1,0:T(8,128)(2,1)S(1)}, bf16[8,64,2048]{2,1,0:T(8,128)(2,1)}, u32[]{:S(2)}) copy-start(bf16[8,64,2048]{2,1,0:T(8,128)(2,1)} %convolution_convert_fusion) | copy-start | bytes 6291460
  233.8 3.9 %copy-start.12 = (bf16[704,2048]{1,0:T(8,128)(2,1)S(1)}, bf16[704,2048]{1,0:T(8,128)(2,1)}, u32[]{:S(2)}) copy-start(bf16[704,2048]{1,0:T(8,128)(2,1)} %copy-done.11) | copy-start | bytes 8650756
  240.8 4.3 %copy-start.14 = (bf16[8,64,2048]{2,1,0:T(8,128)(2,1)S(1)}, bf16[8,64,2048]{2,1,0:T(8,128)(2,1)}, u32[]{:S(2)}) copy-start(bf16[8,64,2048]{2,1,0:T(8,128)(2,1)} %convolution_convert_fusion.1) | copy-start | bytes 6291460
  245.1 3.9 %copy-start.10 = (bf16[704,2048]{1,0:T(8,128)(2,1)S(1)}, bf16[704,2048]{1,0:T(8,128)(2,1)}, u32[]{:S(2)}) copy-start(bf16[704,2048]{1,0:T(8,128)(2,1)} %get-tuple-element.16) | copy-start | bytes 8650756
  254.8 42.8 %copy-start.1 = (bf16[1,2048,512]{2,1,0:T(8,128)(2,1)S(1)}, bf16[1,2048,512]{2,1,0:T(8,128)(2,1)}, u32[]{:S(2)}) copy-start(bf16[1,2048,512]{2,1,0:T(8,128)(2,1)} %param.28) | copy-start | bytes 6291460
  (6 other events, 11.1 us)
